TPU v7x, 32 devices: a whole 2x2x4 slice. The times are simulated.
32 devices in a mesh: wide: 16 (over z, y, core), narrow: 2 (over x).
Axes of the slice: x: 2, y: 2, z: 4, core: 2. Of those that a mesh axis runs over, the one named last changes fastest.
Arguments:
- fields: bfloat16 [32, 48, 4, 128], P(('wide', 'narrow')), may hold values from -6 to 6
- var_ids: int32 [32, 48], P(('wide', 'narrow')), may hold values from 0 to 47, each once within a row
- slot_mask: int32 [32, 48], P(('wide', 'narrow')), may hold values from 0 to 1, as said below
- embed_table: bfloat16 [245760], P(('wide', 'narrow')), may hold values from -3 to 3
- agg_in: bfloat16 [3145728], P(('wide', 'narrow')), may hold values from -0.1875 to 0.1875
- agg_out: bfloat16 [1048576], P(('wide', 'narrow')), may hold values from -0.75 to 0.75
- attn_in: bfloat16 [3145728], P(('wide', 'narrow')), may hold values from -0.1875 to 0.1875
- attn_out: bfloat16 [1048576], P(('wide', 'narrow')), may hold values from -1.5 to 1.5
- mlp_in: bfloat16 [4194304], P(('wide', 'narrow')), may hold values from -0.1875 to 0.1875
- mlp_out: bfloat16 [4194304], P(('wide', 'narrow')), may hold values from -0.125 to 0.125
- vectors: bfloat16 [12288], P(('wide', 'narrow')), may hold values from -4 to 4, as said below
- positions: bfloat16 [131072], P(('wide', 'narrow')), may hold values from -3 to 3
- cotangent: bfloat16 [32, 128, 1024], P(('wide', 'narrow')), may hold values from -6 to 6
Outputs:
- result: bfloat16 [32, 128, 1024], P(('wide', 'narrow'))
- fields_grad: bfloat16 [32, 48, 4, 128], P(('wide', 'narrow'))
- grad_embed_table: float32 [245760], P(('wide', 'narrow'))
- grad_agg_in: float32 [3145728], P(('wide', 'narrow'))
- grad_agg_out: float32 [1048576], P(('wide', 'narrow'))
- grad_attn_in: float32 [3145728], P(('wide', 'narrow'))
- grad_attn_out: float32 [1048576], P(('wide', 'narrow'))
- grad_mlp_in: float32 [4194304], P(('wide', 'narrow'))
- grad_mlp_out: float32 [4194304], P(('wide', 'narrow'))
- grad_vectors: float32 [12288], P(('wide', 'narrow'))
- grad_positions: float32 [131072], P(('wide', 'narrow'))
Inputs may be any that keep to these rules, and one draw needn't show every extreme that they name: `slot_mask`: each sample has 8 to 48 live slots; some sample has exactly 48 and some exactly 8. `var_ids`: each sample's slots name every variable once. `vectors`: rows 1 and 5 lie within 0.6 to 1.4.
All inputs are finite; a program needn't handle non-finite values.
Results may differ from a plain program's by a relative error of at most 0.029.
Values may be sent and summed in bfloat16 or wider, within the bound.
A program may use at most 320 MiB of HBM per device.

v0:
```python
import functools
import math

import jax
import jax.numpy as jnp
from jax import lax
from jax.experimental import pallas as pl
from jax.experimental.pallas import tpu as pltpu
from jax.sharding import PartitionSpec as P

D = 1024
HEADS = 16
FF = 4096
VARS = 48
PATCH_PIXELS = 4
PATCHES = 128
VEC_ROWS = 12

PLANES = 4
CORES = 2
LANES = 128
TILE = 256
SHARED = 2
MESH_IDS = pl.DeviceIdType.MESH
VMEM_BYTES = 66 * 1000 * 1000


norm_eps = 1e-05
masked_score = -1e30
highest_precision = lax.Precision.HIGHEST


def layer_norm(values, gain_row, shift_row):
    centre = jnp.mean(values, -1, keepdims=True)
    centred = values - centre
    spread = jnp.mean(centred * centred, -1, keepdims=True)
    return centred * lax.rsqrt(spread + norm_eps) * gain_row + shift_row


def gelu_exact(values):
    return 0.5 * values * (1.0 + lax.erf(values * 0.7071067811865476))


def softmax_rows(scores):
    highest_score = jnp.max(scores, -1, keepdims=True)
    expo = jnp.exp(scores - highest_score)
    return expo / jnp.sum(expo, -1, keepdims=True)


class Place:
    def __init__(self, wide, narrow):
        self.columns = wide // (PLANES * CORES)
        self.narrow = narrow
        self.devices = wide * narrow
        own = lax.axis_index("wide")
        self.core = own % CORES
        self.y = (own // CORES) % self.columns
        self.z = own // (CORES * self.columns)
        self.x = lax.axis_index("narrow")
        near = 1 + self.z % 2
        far = 3 * (1 - self.z // 2)
        self.planes = (self.z, near, 6 - self.z - near - far, far)

    def wide_of(self, z, y, core):
        return (z * self.columns + y) * CORES + core

    def block(self, z, y, x, core):
        return self.wide_of(z, y, core) * self.narrow + x

    def address(self, z, y, x, core):
        return {"wide": self.wide_of(z, y, core), "narrow": x}

    def other_y(self, step):
        return (self.y + 1 + step) % self.columns

    def other_x(self, step):
        return (self.x + 1 + step) % self.narrow

    def partners(self):
        found = [self.address(z, self.y, self.x, self.core) for z in self.planes[1:]]
        found += [self.address(self.z, self.other_y(i), self.x, self.core) for i in range(self.columns - 1)]
        found += [self.address(self.z, self.y, self.other_x(i), self.core) for i in range(self.narrow - 1)]
        found.append(self.address(self.z, self.y, self.x, 1 - self.core))
        return found

    def greet(self):
        barrier = pltpu.get_barrier_semaphore()
        found = self.partners()
        for partner in found:
            pl.semaphore_signal(barrier, inc=1, device_id=partner, device_id_type=MESH_IDS)
        pl.semaphore_wait(barrier, len(found))


def repeat(count, step):
    if count <= 2:
        for index in range(count):
            step(index)
    else:

        def body(index, carry):
            step(index)
            return carry

        lax.fori_loop(0, count, body, 0)


def lines_to_rows(lines, single, rows):
    count, cols = rows.shape
    each = cols // LANES
    single[: lines.shape[0], :] = lines[...].astype(jnp.float32)
    for at in range(each):
        rows[:, at * LANES : (at + 1) * LANES] = single[pl.ds(at, count, stride=each), :].astype(rows.dtype)


PHASES = (((6,1,0,1),(2,2,0,2)), ((4,2,0,2),(3,4,0,2)), ((3,4,2,4),(5,2,0,2)), ((0,4,0,2),), ((0,4,2,4),), ((1,4,0,2),), ((1,4,2,4),))


COARSE_PHASES = (((6, 1, 0, 1), (2, 2, 0, 2)), ((4, 2, 0, 2), (3, 2, 0, 2)), ((5, 2, 0, 2), (0, 2, 0, 2)), ((1, 2, 0, 2),))
MOST_PIECES = 2048


def phase_parts(widths, devices, phases, coarse):
    found = []
    pieces_in_all = sum(last - first for phase in phases for _, _, first, last in phase)
    for phase in phases if pieces_in_all * devices <= MOST_PIECES else coarse:
        parts = []
        for kind, pieces, first, last in phase:
            width = widths[kind] // pieces
            parts += [(kind, piece * width, width, piece % 2) for piece in range(first, last)]
        found.append(parts)
    return found


def lines_of_variables(devices):
    each = VARS * (PATCH_PIXELS + 1) * D // LANES // devices
    var_lines = (PATCH_PIXELS + 1) * D // LANES
    repeats = math.lcm(each, var_lines)
    return each, repeats // each, repeats // var_lines


def variable_order(devices):
    _, _, period = lines_of_variables(devices)
    return [period * (place % (VARS // period)) + place // (VARS // period) for place in range(VARS)]


def fits(devices):
    return D % (16 * devices) == 0 and VEC_ROWS * D % (LANES * devices) == 0 and PATCHES % devices == 0


def mul(left, right, contract=((1,), (0,)), precision=None):
    return lax.dot_general(
        left, right, (contract, ((), ())), preferred_element_type=jnp.float32, precision=precision
    )


class Forward:
    def __init__(self, devices, weights, small, given, outs, scratch):
        self.devices, self.weights, self.small = devices, weights, small
        self.pixels, self.live = given
        (
            self.table_left,
            self.rows,
            self.keys,
            self.values,
            self.dots,
            self.agg_probs,
            self.mixture_left,
            self.stream,
            self.normed1_left,
            self.projected,
            self.self_probs,
            self.attended_left,
            self.stream1,
            self.normed2_left,
            self.hidden,
            self.activated_left,
        ) = outs
        (
            self.lines,
            self.positions,
            self.query,
            self.table,
            self.spread,
            self.mixture,
            self.normed1,
            self.attended,
            self.normed2,
        ) = scratch

    def tile(self, kind, column):
        weight = self.weights[kind]
        count, rows, _ = weight.shape
        return weight[:, :, pl.ds(column, TILE)].reshape(count * rows, TILE)

    def loop(self, count, step):
        lax.fori_loop(0, count, lambda i, carry: (step(i), carry)[1], 0)

    def turn(self, source, target):
        def one(i):
            at = pl.multiple_of(i * TILE, TILE)
            block = source[:, pl.ds(at, TILE)].astype(jnp.float32)
            target[pl.ds(at, TILE), :] = block.T.astype(jnp.bfloat16)

        self.loop(source.shape[1] // TILE, one)

    def unpack(self):
        devices, tall = self.devices, self.small.shape[1]

        def widen(d):
            self.lines[pl.ds(pl.multiple_of(d * tall, 8), tall), :] = self.small[d].astype(jnp.float32)

        self.loop(devices, widen)
        per_row = D // LANES
        each, span, period = lines_of_variables(devices)
        count = VARS // period
        for p in range(PATCH_PIXELS + 1):
            for b in range(period):
                for c in range(per_row):
                    line = ((PATCH_PIXELS + 1) * b + p) * per_row + c
                    start = tall * (line // each) + line % each
                    self.table[pl.ds(p * VARS + b * count, count), pl.ds(c * LANES, LANES)] = self.lines[
                        pl.ds(start, count, stride=tall * span), :
                    ].astype(jnp.bfloat16)
        first, each = each, VEC_ROWS * per_row // devices
        for row in range(VEC_ROWS):
            for c in range(per_row):
                line = row * per_row + c
                start = tall * (line // each) + first + line % each
                self.rows[pl.ds(row, 1), pl.ds(c * LANES, LANES)] = self.lines[pl.ds(start, 1), :]
        first, rows = first + each, PATCHES // devices
        for row in range(rows):
            for c in range(per_row):
                start = first + row * per_row + c
                self.positions[c, pl.ds(row, devices, stride=rows), :] = self.lines[
                    pl.ds(start, devices, stride=tall), :
                ]

    def table_products(self):
        head = self.rows[0:8, :].astype(jnp.bfloat16)

        def query(i):
            column = pl.multiple_of(i * TILE, TILE)
            found = mul(head, self.tile(2, column)).astype(jnp.bfloat16).astype(jnp.float32)
            self.query[:, pl.ds(column, TILE)] = found
            self.rows[pl.ds(VEC_ROWS, 1), pl.ds(column, TILE)] = found[0:1]

        def key(i):
            column = pl.multiple_of(i * TILE, TILE)
            self.keys[:, pl.ds(column, TILE)] = mul(self.table[...], self.tile(2, D + column))

        def value(i):
            column = pl.multiple_of(i * TILE, TILE)
            self.values[:, pl.ds(column, TILE)] = mul(self.table[...], self.tile(2, 2 * D + column)).astype(
                jnp.bfloat16
            )

        self.loop(D // TILE, query)
        self.loop(D // TILE, key)
        self.loop(D // TILE, value)
        size = D // HEADS
        unit = lax.broadcasted_iota(jnp.int32, (D, LANES), 0)
        head_first = lax.broadcasted_iota(jnp.int32, (D, LANES), 1) * size
        member = jnp.where((unit >= head_first) & (unit < head_first + size), 1.0, 0.0)
        self.dots[...] = mul(self.keys[...] * self.query[0:1, :], member, precision=highest_precision) * size**-0.5

    def aggregate(self):
        size = D // HEADS
        lane = lax.broadcasted_iota(jnp.int32, self.dots.shape, 1)
        low_half = lax.broadcasted_iota(jnp.int32, (PATCHES, LANES), 1) < size

        def pair(g):
            columns = pl.ds(pl.multiple_of(g * LANES, LANES), LANES)
            halves = []
            for i in range(2):
                h = 2 * g + i
                dots = jnp.sum(jnp.where(lane == h, self.dots[...], 0.0), 1, keepdims=True)
                scores = self.pixels[0:VARS, :] * dots[0:VARS]
                for p in range(1, PATCH_PIXELS + 1):
                    here = slice(p * VARS, (p + 1) * VARS)
                    scores = scores + self.pixels[here, :] * dots[here]
                scores = jnp.where(self.live[...] > 0, scores, masked_score)
                expo = jnp.exp(scores - jnp.max(scores, 0, keepdims=True))
                probs = expo / jnp.sum(expo, 0, keepdims=True)
                self.agg_probs[h] = probs
                for p in range(PATCH_PIXELS + 1):
                    here = pl.ds(p * VARS, VARS)
                    self.spread[h, here, :] = (probs * self.pixels[here, :]).astype(jnp.bfloat16)
                halves.append(mul(self.spread[h], self.values[:, columns], ((0,), (0,))))
            self.mixture[:, columns] = jnp.where(low_half, halves[0], halves[1]).astype(jnp.bfloat16)

        self.loop(HEADS // 2, pair)
        self.turn(self.mixture, self.mixture_left)
        table = self.table.shape[0]
        filling = self.table_left.shape[1] - table
        first = lax.broadcasted_iota(jnp.int32, (filling, LANES), 0) == 0
        for c in range(D // LANES):
            columns = slice(c * LANES, (c + 1) * LANES)
            block = jnp.concatenate(
                [self.table[:, columns].astype(jnp.float32), jnp.where(first, self.rows[0:1, columns], 0.0)], 0
            )
            self.table_left[columns, :] = block.T.astype(jnp.bfloat16)

    def join(self):
        def one(i):
            columns = pl.ds(pl.multiple_of(i * TILE, TILE), TILE)
            shift = jnp.concatenate([self.positions[2 * i], self.positions[2 * i + 1]], 1)
            self.stream[:, columns] = mul(self.mixture[...], self.tile(4, pl.multiple_of(i * TILE, TILE))) + shift

        self.loop(D // TILE, one)
        self.normed1[...] = layer_norm(self.stream[...], self.rows[1:2, :], self.rows[2:3, :]).astype(jnp.bfloat16)
        self.turn(self.normed1, self.normed1_left)

    def project(self):
        def with_bias(i):
            column = pl.multiple_of(i * TILE, TILE)
            columns = pl.ds(column, TILE)
            found = mul(self.normed1[...], self.tile(3, column)) + self.rows[3:4, columns]
            self.projected[:, columns] = found.astype(jnp.bfloat16)

        def plain(i):
            column = pl.multiple_of(D + i * TILE, TILE)
            self.projected[:, pl.ds(column, TILE)] = mul(self.normed1[...], self.tile(3, column)).astype(jnp.bfloat16)

        self.loop(D // TILE, with_bias)
        self.loop(2 * D // TILE, plain)

    def attend(self):
        size = D // HEADS
        low_half = lax.broadcasted_iota(jnp.int32, (PATCHES, LANES), 1) < size

        def pair(g):
            column = pl.multiple_of(g * LANES, LANES)
            queries, keys, values = (self.projected[:, pl.ds(third * D + column, LANES)] for third in range(3))
            halves = []
            for i in range(2):
                masked = jnp.where(low_half if i == 0 else ~low_half, queries.astype(jnp.float32), 0.0)
                scores = mul(masked.astype(jnp.bfloat16), keys, ((1,), (1,))) * size**-0.5
                peak = jnp.max(scores, -1, keepdims=True)
                lse = peak + jnp.log(jnp.sum(jnp.exp(scores - peak), -1, keepdims=True))
                probs = jnp.exp(scores - lse)
                self.self_probs[2 * g + i] = probs
                halves.append(mul(probs.astype(jnp.bfloat16), values))
            self.attended[:, pl.ds(column, LANES)] = jnp.where(low_half, halves[0], halves[1]).astype(jnp.bfloat16)

        self.loop(HEADS // 2, pair)

    def join_attended(self):
        def one(i):
            columns = pl.ds(pl.multiple_of(i * TILE, TILE), TILE)
            found = self.stream[:, columns] + mul(self.attended[...], self.tile(5, pl.multiple_of(i * TILE, TILE)))
            self.stream1[:, columns] = found + self.rows[4:5, columns]

        self.loop(D // TILE, one)
        self.normed2[...] = layer_norm(self.stream1[...], self.rows[5:6, :], self.rows[6:7, :]).astype(jnp.bfloat16)
        self.turn(self.attended, self.attended_left)
        self.turn(self.normed2, self.normed2_left)

    def feed(self):
        per_row = D // TILE

        def one(i):
            column = pl.multiple_of(i * TILE, TILE)
            columns = pl.ds(column, TILE)
            shift = self.rows[pl.ds(8 + i // per_row, 1), pl.ds(pl.multiple_of((i % per_row) * TILE, TILE), TILE)]
            found = mul(self.normed2[...], self.tile(0, column)) + shift
            self.hidden[:, columns] = found
            self.activated_left[columns, :] = gelu_exact(found).T.astype(jnp.bfloat16)

        self.loop(FF // TILE, one)

    def after(self, phase):
        return {
            0: (self.unpack, self.table_products, self.aggregate),
            1: (self.join,),
            2: (self.project, self.attend, self.join_attended),
            4: (self.feed,),
        }.get(phase, ())


def norm_back(values, grad, gain_row):
    centred = values - jnp.mean(values, -1, keepdims=True)
    inverse = lax.rsqrt(jnp.mean(centred * centred, -1, keepdims=True) + norm_eps)
    unit = centred * inverse
    back = grad * gain_row
    down = inverse * (back - jnp.mean(back, -1, keepdims=True) - unit * jnp.mean(back * unit, -1, keepdims=True))
    return down, jnp.sum(grad * unit, 0, keepdims=True), jnp.sum(grad, 0, keepdims=True)


class Backward:
    def __init__(self, devices, narrow, weights, streamed, given, outs, rights, scratch):
        self.devices, self.narrow, self.weights, self.rights = devices, narrow, weights, rights
        self.hidden, self.activated = streamed
        (
            self.rows,
            self.keys,
            self.values,
            self.dots,
            self.agg_probs,
            self.stream,
            self.projected,
            self.self_probs,
            self.stream1,
            self.pixels,
            self.cotangent,
        ) = given
        self.result, self.grad_pixels = outs
        (
            self.pack,
            self.tall_tiles,
            self.flat_tiles,
            self.hidden_tiles,
            self.activated_tiles,
            self.down,
            self.grad_stream1,
            self.narrow_grad,
            self.grad_rows,
            self.grad_dots,
            self.positions,
            self.lines,
            self.tile_sem,
        ) = scratch

    def loop(self, count, step):
        lax.fori_loop(0, count, lambda i, carry: (step(i), carry)[1], 0)

    def rolling(self, count, copies, step, unrolled=False):
        for copy in copies(0, 0):
            copy.start()

        def one(i):
            slot = i % 2
            if unrolled:
                following = copies(i + 1, 1 - slot) if i + 1 < count else []
                for copy in following:
                    copy.start()
            else:

                def ahead():
                    for copy in copies(i + 1, 1 - slot):
                        copy.start()

                pl.when(i + 1 < count)(ahead)
            for copy in copies(i, slot):
                copy.wait()
            step(i, slot)

        if unrolled:
            for i in range(count):
                one(i)
        else:
            self.loop(count, one)

    def row_tiles(self, kind, step, unrolled=False):
        weight = self.weights[kind]
        _, rows, cols = weight.shape
        blocks = TILE // rows

        def copies(i, slot):
            target = self.flat_tiles.at[slot, :, :, pl.ds(0, cols)]
            return [pltpu.make_async_copy(weight.at[pl.ds(i * blocks, blocks)], target, self.tile_sem.at[slot, 0])]

        def one(i, slot):
            column = i * TILE if unrolled else pl.multiple_of(i * TILE, TILE)
            step(column, lambda at, width: self.flat_tiles[slot, :, :, pl.ds(at, width)].reshape(TILE, width))

        self.rolling(D // TILE, copies, one, unrolled)

    def through(self, kind, left, target):
        cols = self.weights[kind].shape[2]

        def one(column, weight):
            found = mul(left[...], weight(0, cols), ((1,), (1,)))
            target[:, pl.ds(column, TILE)] = found.astype(target.dtype)

        self.row_tiles(kind, one)

    def right(self, kind):
        return self.rights[kind].at[pl.ds(0, PATCHES)]

    def feed(self):
        weight = self.weights[1]
        blocks = TILE // weight.shape[1]
        per_row = D // TILE
        grad_hidden = self.right(0)

        def copies(i, slot):
            columns = pl.ds(i * TILE if isinstance(i, int) else pl.multiple_of(i * TILE, TILE), TILE)
            return [
                pltpu.make_async_copy(
                    weight.at[pl.ds(i * blocks, blocks)], self.tall_tiles.at[slot], self.tile_sem.at[slot, 0]
                ),
                pltpu.make_async_copy(
                    self.hidden.at[:, columns], self.hidden_tiles.at[slot], self.tile_sem.at[slot, 1]
                ),
                pltpu.make_async_copy(
                    self.activated.at[columns], self.activated_tiles.at[slot], self.tile_sem.at[slot, 2]
                ),
            ]

        self.down[...] = self.stream1[...] + self.rows[7:8, :]

        def one(i, slot):
            rows = self.tall_tiles[slot].reshape(TILE, D)
            self.down[...] += mul(self.activated_tiles[slot], rows, ((0,), (0,)))
            grad = mul(self.cotangent[...], rows, ((1,), (1,)))
            values = self.hidden_tiles[slot]
            slope = 0.5 * (1.0 + lax.erf(values * 0.7071067811865476))
            slope = slope + values * jnp.exp(-0.5 * values * values) * 0.3989422804014327
            grad = (grad * slope).astype(jnp.bfloat16)
            grad_hidden[:, pl.ds(pl.multiple_of(i * TILE, TILE), TILE)] = grad
            there = pl.ds(pl.multiple_of((i % per_row) * TILE, TILE), TILE)
            self.grad_rows[pl.ds(8 + i // per_row, 1), there] = jnp.sum(grad.astype(jnp.float32), 0, keepdims=True)

        self.rolling(FF // TILE, copies, one)
        self.result[...] = self.down[...].astype(jnp.bfloat16)

    def norm2(self):
        self.through(0, self.right(0), self.down)
        grad = self.cotangent[...].astype(jnp.float32)
        back, gain, shift = norm_back(self.stream1[...], self.down[...], self.rows[5:6, :])
        self.grad_rows[5:6, :] = gain
        self.grad_rows[6:7, :] = shift
        self.grad_rows[7:8, :] = jnp.sum(grad, 0, keepdims=True)
        total = grad + back
        self.grad_stream1[...] = total
        branch = total.astype(jnp.bfloat16)
        self.right(5)[...] = branch
        self.grad_rows[4:5, :] = jnp.sum(branch.astype(jnp.float32), 0, keepdims=True)

    def attend(self):
        self.through(5, self.right(5), self.narrow_grad)
        size = D // HEADS
        scale = size**-0.5
        low_half = lax.broadcasted_iota(jnp.int32, (PATCHES, LANES), 1) < size
        grad_projected = self.right(3)

        def pair(g):
            column = pl.multiple_of(g * LANES, LANES)
            queries, keys, values = (self.projected[:, pl.ds(third * D + column, LANES)] for third in range(3))
            grad = self.narrow_grad[:, pl.ds(column, LANES)]
            halves = []
            for i in range(2):
                masked = jnp.where(low_half if i == 0 else ~low_half, grad.astype(jnp.float32), 0.0)
                probs = self.self_probs[2 * g + i]
                back = mul(masked.astype(jnp.bfloat16), values, ((1,), (1,)))
                scores = probs * (back - jnp.sum(probs * back, -1, keepdims=True))
                scores = scores.astype(jnp.bfloat16)
                halves.append(
                    (
                        mul(scores, keys) * scale,
                        mul(scores, queries, ((0,), (0,))) * scale,
                        mul(probs.astype(jnp.bfloat16), grad, ((0,), (0,))),
                    )
                )
            for third in range(3):
                found = jnp.where(low_half, halves[0][third], halves[1][third])
                grad_projected[:, pl.ds(third * D + column, LANES)] = found.astype(jnp.bfloat16)

        self.loop(HEADS // 2, pair)
        self.grad_rows[3:4, :] = jnp.sum(grad_projected[:, pl.ds(0, D)].astype(jnp.float32), 0, keepdims=True)

    def norm1(self):
        self.through(3, self.right(3), self.down)
        back, gain, shift = norm_back(self.stream[...], self.down[...], self.rows[1:2, :])
        self.grad_rows[1:2, :] = gain
        self.grad_rows[2:3, :] = shift
        total = self.grad_stream1[...] + back
        self.right(4)[...] = total.astype(jnp.bfloat16)
        for c in range(D // LANES):
            self.positions[c] = total[:, c * LANES : (c + 1) * LANES]

    def aggregate(self):
        self.through(4, self.right(4), self.narrow_grad)
        size = D // HEADS
        scale = size**-0.5
        table = VARS * (PATCH_PIXELS + 1)
        lane = lax.broadcasted_iota(jnp.int32, self.dots.shape, 1)
        low_half = lax.broadcasted_iota(jnp.int32, (PATCHES, LANES), 1) < size
        low_table = lax.broadcasted_iota(jnp.int32, (table, LANES), 1) < size
        right = self.rights[SHARED]
        self.grad_dots[...] = jnp.zeros_like(self.grad_dots)
        self.grad_pixels[...] = jnp.zeros_like(self.grad_pixels)
        slabs = [pl.ds(p * VARS, VARS) for p in range(PATCH_PIXELS + 1)]

        def pair(g):
            column = pl.multiple_of(g * LANES, LANES)
            values = self.values[:, pl.ds(column, LANES)]
            grad = self.narrow_grad[:, pl.ds(column, LANES)]
            halves = []
            for i in range(2):
                h = 2 * g + i
                masked = jnp.where(low_half if i == 0 else ~low_half, grad.astype(jnp.float32), 0.0)
                back = mul(values, masked.astype(jnp.bfloat16), ((1,), (1,)))
                probs = self.agg_probs[h]
                grad_probs = back[0:VARS] * self.pixels[slabs[0], :]
                for p in range(1, PATCH_PIXELS + 1):
                    grad_probs = grad_probs + back[p * VARS : (p + 1) * VARS] * self.pixels[slabs[p], :]
                scores = probs * (grad_probs - jnp.sum(probs * grad_probs, 0, keepdims=True))
                dots = jnp.sum(jnp.where(lane == h, self.dots[...], 0.0), 1, keepdims=True)
                spread = []
                for p in range(PATCH_PIXELS + 1):
                    rows = slice(p * VARS, (p + 1) * VARS)
                    if p < PATCH_PIXELS:
                        self.grad_pixels[slabs[p], :] += scores * dots[rows] + probs * back[rows]
                    found = jnp.sum(self.pixels[slabs[p], :] * scores, 1, keepdims=True) * scale
                    self.grad_dots[slabs[p], :] += jnp.where(lane[rows] == h, found, 0.0)
                    spread.append((probs * self.pixels[slabs[p], :]).astype(jnp.bfloat16))
                halves.append(mul(jnp.concatenate(spread, 0), grad))
            found = jnp.where(low_table, halves[0], halves[1]).astype(jnp.bfloat16)
            right[pl.ds(0, table), pl.ds(2 * D + column, LANES)] = found

        self.loop(HEADS // 2, pair)
        unit = lax.broadcasted_iota(jnp.int32, (D, LANES), 0)
        head_first = lax.broadcasted_iota(jnp.int32, (D, LANES), 1) * size
        member = jnp.where((unit >= head_first) & (unit < head_first + size), 1.0, 0.0)
        wide = mul(self.grad_dots[...], member, ((1,), (1,)), highest_precision)
        query = jnp.sum(wide * self.keys[...], 0, keepdims=True)
        depth = right.shape[0]
        right[pl.ds(0, table), pl.ds(0, D)] = jnp.zeros((table, D), jnp.bfloat16)
        right[pl.ds(0, table), pl.ds(D, D)] = (wide * self.rows[VEC_ROWS : VEC_ROWS + 1, :]).astype(jnp.bfloat16)
        first = lax.broadcasted_iota(jnp.int32, (depth - table, D), 0) == 0
        right[pl.ds(table, depth - table), pl.ds(0, D)] = jnp.where(first, query, 0.0).astype(jnp.bfloat16)
        right[pl.ds(table, depth - table), pl.ds(D, 2 * D)] = jnp.zeros((depth - table, 2 * D), jnp.bfloat16)
        self.grad_rows[VEC_ROWS : VEC_ROWS + 1, :] = query

    def small(self):
        devices = self.devices
        tall = self.lines.shape[0] // devices
        per_row = D // LANES
        table = VARS * (PATCH_PIXELS + 1)
        each, span, period = lines_of_variables(devices)
        count = VARS // period
        right = self.rights[SHARED]

        def one(column, weight):
            back = mul(right[pl.ds(0, table), pl.ds(D, 2 * D)], weight(D, 2 * D), ((1,), (1,)))
            query = jnp.broadcast_to(self.grad_rows[VEC_ROWS : VEC_ROWS + 1, :], (8, D))
            row = mul(query, weight(0, D).astype(jnp.float32), ((1,), (1,)), highest_precision)
            self.grad_rows[0:1, column : column + TILE] = row[0:1]
            for p in range(PATCH_PIXELS + 1):
                for b in range(period):
                    for c in range(TILE // LANES):
                        line = ((PATCH_PIXELS + 1) * b + p) * per_row + column // LANES + c
                        start = tall * (line // each) + line % each
                        first = p * VARS + b * count
                        self.lines[pl.ds(start, count, stride=tall * span), :] = back[
                            first : first + count, c * LANES : (c + 1) * LANES
                        ]

        self.row_tiles(SHARED, one, True)
        first, each = each, VEC_ROWS * per_row // devices
        for row in range(VEC_ROWS):
            for c in range(per_row):
                line = row * per_row + c
                start = tall * (line // each) + first + line % each
                self.lines[pl.ds(start, 1), :] = self.grad_rows[pl.ds(row, 1), pl.ds(c * LANES, LANES)]
        first, rows = first + each, PATCHES // devices
        for row in range(rows):
            for c in range(per_row):
                start = first + row * per_row + c
                self.lines[pl.ds(start, devices, stride=tall), :] = self.positions[
                    c, pl.ds(row, devices, stride=rows), :
                ]
        for line in range(first + rows * per_row, tall):
            self.lines[pl.ds(line, devices, stride=tall), :] = jnp.zeros((devices, LANES), jnp.float32)

        cores = self.pack.shape[0]

        def one_block(d):
            block = self.lines[pl.ds(pl.multiple_of(d * tall, 8), tall), :].astype(jnp.bfloat16)
            self.pack[(d // self.narrow) % cores, d // (cores * self.narrow) * self.narrow + d % self.narrow] = block

        self.loop(devices, one_block)

    def before(self, phase):
        return {
            2: ((self.feed,), (0,)),
            4: ((self.norm2, self.attend), (5, 3)),
            5: ((self.norm1,), (4,)),
            6: ((self.aggregate,), (SHARED,)),
            7: ((self.small,), (6,)),
        }.get(phase, ((), ()))


LOADED = (0, 2, 3, 4, 5, 6)


def forward_shapes():
    low, full = jnp.bfloat16, jnp.float32
    table = VARS * (PATCH_PIXELS + 1)
    return [
        jax.ShapeDtypeStruct(shape, kind)
        for shape, kind in (
            ((D, 2 * LANES), low),
            ((16, D), full),
            ((table, D), full),
            ((table, D), low),
            ((table, LANES), full),
            ((HEADS, VARS, PATCHES), full),
            ((D, PATCHES), low),
            ((PATCHES, D), full),
            ((D, PATCHES), low),
            ((PATCHES, 3 * D), low),
            ((HEADS, PATCHES, PATCHES), full),
            ((D, PATCHES), low),
            ((PATCHES, D), full),
            ((D, PATCHES), low),
            ((PATCHES, FF), full),
            ((FF, PATCHES), low),
        )
    ]


def gather_kernel(widths, wide, narrow, fused, *refs):
    kinds = len(widths)
    refs = list(refs)

    def take(count):
        found = refs[:count]
        del refs[:count]
        return found

    flats, given = take(kinds), take(2 if fused else 0)
    whole, outs = take(kinds), take(len(forward_shapes()) if fused else 0)
    shards = take(kinds)
    loaded = dict(zip(LOADED, take(len(LOADED) if fused else 0)))
    scratch = take(9 if fused else 0)
    load_sem = take(1 if fused else 0)
    single, send_sem, relay_sem, recv_sem, own_sem = refs
    forward = Forward(wide * narrow, loaded, loaded[6], given, outs, scratch) if fused else None
    here = Place(wide, narrow)
    for kind in range(kinds):
        lines_to_rows(flats[kind], single, shards[kind])
    here.greet()
    own_slot = here.block(here.z, here.y, here.x, here.core)
    for kind in range(kinds):
        pltpu.make_async_copy(shards[kind], whole[kind].at[own_slot], own_sem.at[kind]).start()
    phases, number = [], 0
    for parts in phase_parts(widths, here.devices, PHASES, COARSE_PHASES):
        phases.append([(number + i,) + part for i, part in enumerate(parts)])
        number += len(parts)

    def view(part, slot):
        kind, at, width = part[1:4]
        return whole[kind].at[slot, :, pl.ds(at, width)]

    def push(part, slot, target, source=None):
        pltpu.make_async_remote_copy(
            src_ref=view(part, slot) if source is None else source,
            dst_ref=view(part, slot),
            send_sem=send_sem.at[part[1]],
            recv_sem=recv_sem.at[part[0], slot],
            device_id=target,
            device_id_type=MESH_IDS,
        ).start()

    def arrived(part, slot):
        pltpu.make_async_copy(view(part, slot), view(part, slot), recv_sem.at[part[0], slot]).wait()

    def along(y_axis):
        if y_axis:
            return here.columns - 1, lambda i: here.address(here.z, here.other_y(i), here.x, here.core)
        return here.narrow - 1, lambda i: here.address(here.z, here.y, here.other_x(i), here.core)

    def to_axis(part, y_axis, slot, source=None):
        count, address = along(y_axis)
        repeat(count, lambda i: push(part, slot, address(i), source))

    def to_sibling(part, slot, source=None):
        push(part, slot, here.address(here.z, here.y, here.x, 1 - here.core), source)

    across = (here.z + 2) % PLANES
    beside = here.z + 1 - 2 * (here.z % 2)
    beyond = (beside + 2) % PLANES

    middle = (here.z + 1) // 2 == 1
    facing = PLANES - 1 - here.z

    def relay(part, slot, z, source=None):
        pltpu.make_async_remote_copy(
            src_ref=view(part, slot) if source is None else source,
            dst_ref=view(part, slot),
            send_sem=relay_sem.at[part[1]],
            recv_sem=recv_sem.at[part[0], slot],
            device_id=here.address(z, here.y, here.x, here.core),
            device_id_type=MESH_IDS,
        ).start()

    def pass_on(parts, z):
        slot = here.block(z, here.y, here.x, here.core)
        for part in parts:

            def one(part=part):
                arrived(part, slot)
                relay(part, slot, beside)

            pl.when(middle)(one)

    def send_own(parts):
        for part in parts:
            source = shards[part[1]].at[:, pl.ds(part[2], part[3])]
            for y_axis in (part[4] == 0, part[4] != 0):
                to_axis(part, y_axis, own_slot, source)
            relay(part, own_slot, beside, source)
            pl.when(middle)(lambda part=part, source=source: relay(part, own_slot, facing, source))
            to_sibling(part, own_slot, source)

    def first_hop(parts, z, passes=True):
        slot = here.block(z, here.y, here.x, here.core)
        for part in parts:
            if passes:
                arrived(part, slot)
                target = facing if z is beside else beside
                pl.when(middle)(lambda part=part: relay(part, slot, target))
            else:
                pl.when(jnp.logical_not(middle))(lambda part=part: arrived(part, slot))
            for y_axis in (part[4] == 0, part[4] != 0):
                to_axis(part, y_axis, slot)
            to_sibling(part, slot)

    def second_hop(parts, z, crosses):
        for part in parts:
            y_axis = part[4] == 0

            def along_first(i):
                slot = (
                    here.block(z, here.other_y(i), here.x, here.core)
                    if y_axis
                    else here.block(z, here.y, here.other_x(i), here.core)
                )
                arrived(part, slot)
                if crosses:
                    to_axis(part, not y_axis, slot)
                to_sibling(part, slot)

            repeat(along(y_axis)[0], along_first)

    def other_second_hop(parts, z):
        for part in parts:
            y_axis = part[4] != 0

            def along_second(i):
                slot = (
                    here.block(z, here.other_y(i), here.x, here.core)
                    if y_axis
                    else here.block(z, here.y, here.other_x(i), here.core)
                )
                arrived(part, slot)
                to_sibling(part, slot)

            repeat(along(y_axis)[0], along_second)

    def third_hop(parts, z, crosses):
        for part in parts:

            def one(i, j):
                slot = here.block(z, here.other_y(i), here.other_x(j), here.core)
                arrived(part, slot)
                if crosses:
                    push(part, slot, here.address(beside, here.y, here.x, here.core))
                to_sibling(part, slot)

            repeat(here.columns - 1, lambda i: repeat(here.narrow - 1, lambda j: one(i, j)))

    def stage_b(parts):
        first_hop(parts, beside)
        pass_on(parts, beyond)
        second_hop(parts, here.z, True)

    def stage_c(parts):
        first_hop(parts, across)
        third_hop(parts, here.z, True)
        other_second_hop(parts, here.z)

    def stage_d(parts):
        second_hop(parts, across, True)
        first_hop(parts, beyond, False)
        other_second_hop(parts, across)
        second_hop(parts, beside, False)
        other_second_hop(parts, beside)

    def stage_e(parts):
        third_hop(parts, across, True)
        third_hop(parts, beside, False)
        second_hop(parts, beyond, False)
        other_second_hop(parts, beyond)
        third_hop(parts, beyond, False)

    def stage_f(parts):
        def from_sibling(index):
            per_plane = here.columns * here.narrow
            plane, rest = index // per_plane, index % per_plane
            slot = here.block(plane, rest // here.narrow, rest % here.narrow, 1 - here.core)
            for part in parts:
                arrived(part, slot)

        lax.fori_loop(0, here.devices // CORES, lambda i, c: (from_sibling(i), c)[1], 0)

    settled = set()

    def settle_own(kind):
        if kind not in settled:
            pltpu.make_async_copy(shards[kind], whole[kind].at[own_slot], own_sem.at[kind]).wait()
        settled.add(kind)

    def load(part):
        there = pl.ds(part[2], part[3])
        return pltpu.make_async_copy(
            whole[part[1]].at[:, :, there], loaded[part[1]].at[:, :, there], load_sem[0].at[part[0]]
        )

    def stage_load(parts):
        for part in parts:
            if fused and part[1] in LOADED:
                settle_own(part[1])
                load(part).start()

    def stage_compute(parts):
        for part in parts:
            if fused and part[1] in LOADED:
                load(part).wait()
        if fused:
            for work in forward.after(phases.index(parts)):
                work()

    stages = (send_own, stage_b, stage_c, stage_d, stage_e, stage_f, stage_load, stage_compute)
    lags = (0, 1, 2, 3, 4, 5, 5, 6)
    for step in range(len(phases) + lags[-1]):
        for stage in (5, 4, 3, 2, 1, 0, 6, 7):
            if 0 <= step - lags[stage] < len(phases):
                stages[stage](phases[step - lags[stage]])
    for kind in range(kinds):
        settle_own(kind)
        sent = whole[kind].at[pl.ds(0, here.devices - PLANES)]
        pltpu.make_async_copy(sent, sent, send_sem.at[kind]).wait()
        once = whole[kind].at[pl.ds(0, 1)]
        pltpu.make_async_copy(once, once, relay_sem.at[kind]).wait()

        def relayed(kind=kind):
            four = whole[kind].at[pl.ds(0, 4)]
            pltpu.make_async_copy(four, four, relay_sem.at[kind]).wait()

        pl.when(middle)(relayed)


def gather_all(flats, widths, wide, narrow, given=()):
    devices = wide * narrow
    kinds = len(flats)
    fused = bool(given)
    shapes = [(flat.size // width, width) for flat, width in zip(flats, widths)]
    lines = [flat.reshape(-1, LANES) for flat in flats]
    parts = sum(len(phase) for phase in phase_parts(widths, devices, PHASES, COARSE_PHASES))
    results = forward_shapes() if fused else []
    scratch = [pltpu.VMEM(s, f.dtype) for s, f in zip(shapes, flats)]
    if fused:
        scratch += [pltpu.VMEM((devices,) + shapes[kind], flats[kind].dtype) for kind in LOADED]
        scratch += [
            pltpu.VMEM((devices * shapes[6][0], LANES), jnp.float32),
            pltpu.VMEM((D // LANES, PATCHES, LANES), jnp.float32),
            pltpu.VMEM((8, D), jnp.float32),
            pltpu.VMEM((VARS * (PATCH_PIXELS + 1), D), jnp.bfloat16),
            pltpu.VMEM((HEADS, VARS * (PATCH_PIXELS + 1), PATCHES), jnp.bfloat16),
            pltpu.VMEM((PATCHES, D), jnp.bfloat16),
            pltpu.VMEM((PATCHES, D), jnp.bfloat16),
            pltpu.VMEM((PATCHES, D), jnp.bfloat16),
            pltpu.VMEM((PATCHES, D), jnp.bfloat16),
            pltpu.SemaphoreType.DMA((parts,)),
        ]
    scratch += [
        pltpu.VMEM((max(line.shape[0] for line in lines), LANES), jnp.float32),
        pltpu.SemaphoreType.DMA((kinds,)),
        pltpu.SemaphoreType.DMA((kinds,)),
        pltpu.SemaphoreType.DMA((parts, devices)),
        pltpu.SemaphoreType.DMA((kinds,)),
    ]
    found = pl.pallas_call(
        functools.partial(gather_kernel, widths, wide, narrow, fused),
        out_shape=[jax.ShapeDtypeStruct((devices,) + s, f.dtype) for s, f in zip(shapes, flats)] + results,
        in_specs=[pl.BlockSpec(memory_space=pltpu.VMEM)] * (kinds + len(given)),
        out_specs=[pl.BlockSpec(memory_space=pl.ANY)] * kinds
        + [pl.BlockSpec(memory_space=pltpu.VMEM)] * len(results),
        scratch_shapes=scratch,
        compiler_params=pltpu.CompilerParams(
            collective_id=0, has_side_effects=True, vmem_limit_bytes=VMEM_BYTES
        ),
        name="gather_all",
    )(*lines, *given)
    return found[:kinds], found[kinds:]


def add_up(target, sources):
    rows, cols = target.shape
    high = min(rows, 16)
    wide_step = next(w for w in (1024, 768, 512, 256, LANES) if cols % w == 0)

    def tile(index, carry):
        here = pl.ds(pl.multiple_of(index * high, high), high)
        for at in range(0, cols, wide_step):
            there = pl.ds(at, wide_step)
            total = sources[0][here, there].astype(jnp.float32)
            for source in sources[1:]:
                total = total + source[here, there].astype(jnp.float32)
            target[here, there] = total.astype(target.dtype)
        return carry

    lax.fori_loop(0, rows // high, tile, 0)


def add_up_lines(lines, shape, first, sources):
    rows, cols = shape
    width = sources[0].shape[1]
    high = min(rows, 16)
    each = cols // LANES

    def tile(index, carry):
        here = pl.ds(pl.multiple_of(index * high, high), high)
        for at in range(width // LANES):
            there = pl.ds(at * LANES, LANES)
            total = sources[0][here, there].astype(jnp.float32)
            for source in sources[1:]:
                total = total + source[here, there].astype(jnp.float32)
            lines[pl.ds(index * (high * each) + first // LANES + at, high, stride=each), :] = total
        return carry

    lax.fori_loop(0, rows // high, tile, 0)


SUM_PHASES = (
    ((1, 4, 0, 2),),
    ((1, 4, 2, 4),),
    ((0, 4, 0, 2),),
    ((0, 4, 2, 4),),
    ((5, 2, 0, 2), (3, 4, 0, 2)),
    ((3, 4, 2, 4), (4, 2, 0, 2)),
    ((2, 4, 0, 2),),
    ((2, 4, 2, 4), (6, 1, 0, 1)),
)
COARSE_SUM_PHASES = (((1, 2, 0, 2),), ((0, 2, 0, 2),), ((5, 2, 0, 2), (3, 2, 0, 2), (4, 2, 0, 2)), ((2, 2, 0, 2), (6, 1, 0, 1)))


BACK_GIVEN = 11
BACK_SCRATCH = 13


def scatter_kernel(direct, shapes, wide, narrow, fused, *refs):
    kinds = len(shapes)
    refs = list(refs)

    def take(count):
        found = refs[:count]
        del refs[:count]
        return found

    if fused:
        inputs = [take(2) if kind == 1 else take(1) if direct[kind] else [] for kind in range(kinds)]
    else:
        inputs = [take(2) if direct[kind] else take(1) for kind in range(kinds)]
    weights, streamed, given = (take(count if fused else 0) for count in (6, 2, BACK_GIVEN))
    sums = take(kinds)
    outs = take(2 if fused else 0)
    own, second, first, planes, cross = (take(kinds) for _ in range(5))
    local = [take(3) if direct[kind] and kind == SHARED else take(2) if direct[kind] else take(1) for kind in range(kinds)]
    scratch = take(BACK_SCRATCH if fused else 0)
    send_sem, near_send_sem, own_sem, near_sem, second_sem, first_sem, plane_sem, cross_sem = refs
    backward = None
    if fused:
        inputs[6] = [scratch[0]]
        rights = [local[kind][1] if direct[kind] else None for kind in range(kinds)]
        backward = Backward(wide * narrow, narrow, weights, streamed, given, outs, rights, scratch)
    here = Place(wide, narrow)
    here.greet()
    y_count, x_count = here.columns, here.narrow
    half = here.devices // CORES
    sibling = here.address(here.z, here.y, here.x, 1 - here.core)
    across = (here.z + 2) % PLANES
    beside = here.z + 1 - 2 * (here.z % 2)
    phases, number = [], 0
    for parts in phase_parts([s[1] for s in shapes], here.devices, SUM_PHASES, COARSE_SUM_PHASES):
        phases.append([(number + i,) + part for i, part in enumerate(parts)])
        number += len(parts)

    def spot(z, y, x):
        return (z * y_count + y) * x_count + x

    def tokens_of(kind):
        return local[kind][1].shape[0] // (1 if kind == SHARED else 2)

    def made_here(kind):
        return fused and kind != 1

    def mine_left(kind):
        low = pl.ds(0, local[kind][0].shape[2] if kind == SHARED else tokens_of(kind))
        return [
            pltpu.make_async_copy(
                inputs[kind][0].at[:, here.core], local[kind][0].at[:, :, low], own_sem.at[kind, 0]
            )
        ]

    def mine_right(kind):
        if not direct[kind]:
            return [pltpu.make_async_copy(inputs[kind][0].at[here.core], own[kind], own_sem.at[kind, 0])]
        if made_here(kind):
            return []
        low = pl.ds(0, tokens_of(kind))
        return [pltpu.make_async_copy(inputs[kind][1], local[kind][1].at[low], own_sem.at[kind, 1])]

    def remote(kind, i, source, target):
        return pltpu.make_async_remote_copy(
            src_ref=source,
            dst_ref=target,
            send_sem=near_send_sem.at[kind, i],
            recv_sem=near_sem.at[kind, i],
            device_id=sibling,
            device_id_type=MESH_IDS,
        )

    def theirs_left(kind):
        if kind == SHARED:
            return []
        high = pl.ds(tokens_of(kind), tokens_of(kind))
        return [remote(kind, 0, inputs[kind][0].at[:, 1 - here.core], local[kind][0].at[:, :, high])]

    def theirs_right(kind):
        if not direct[kind]:
            return [remote(kind, 0, inputs[kind][0].at[1 - here.core], local[kind][0])]
        tokens = tokens_of(kind)
        source = local[kind][1].at[pl.ds(0, tokens)] if made_here(kind) else inputs[kind][1]
        if kind == SHARED:
            return [remote(kind, 1, source, local[kind][2])]
        return [remote(kind, 1, source, local[kind][1].at[pl.ds(tokens, tokens)])]

    def fetch_left(kind):
        if direct[kind]:
            for copy in mine_left(kind) + theirs_left(kind):
                copy.start()

    def fetch_right(kind):
        for copy in mine_right(kind) + theirs_right(kind):
            copy.start()

    def fetched(kind):
        for copy in (mine_left(kind) if direct[kind] else []) + mine_right(kind):
            copy.wait()
        for copy in (theirs_left(kind) if direct[kind] else []) + theirs_right(kind):
            copy.wait_recv()
        if direct[kind] and kind == SHARED:
            add_up(local[kind][2], [local[kind][1], local[kind][2]])

    def multiply(part):
        _, kind, at, width, _ = part
        if not direct[kind]:
            return
        left, right = local[kind][0], local[kind][-1]
        groups, rows, depth = left.shape
        take_groups = min(groups, max(1, 512 // rows))
        block_rows = shapes[kind][0]
        slots = take_groups * rows // block_rows
        steps = groups // take_groups

        def one(index, carry):
            column = pl.multiple_of(at + (index // steps) * TILE, TILE)
            group = index % steps
            factor = left[pl.ds(group * take_groups, take_groups), :, :].reshape(take_groups * rows, depth)
            block = jnp.dot(factor, right[:, pl.ds(column, TILE)], preferred_element_type=jnp.float32)
            own[kind][pl.ds(group * slots, slots), :, pl.ds(column, TILE)] = block.astype(jnp.bfloat16).reshape(
                slots, block_rows, TILE
            )
            return carry

        lax.fori_loop(0, steps * (width // TILE), one, 0)

    def view(buffer, part, place):
        return buffer[part[1]].at[place, :, pl.ds(part[2], part[3])]

    def landed(buffer, part, place, sem):
        pltpu.make_async_copy(view(buffer, part, place), view(buffer, part, place), sem.at[part[0], place]).wait()
        return view(buffer, part, place)

    def terms_of(part, slot):
        found = [view(own, part, slot)]
        if not direct[part[1]]:
            found.append(view(local_near, part, slot))
        return found

    local_near = [refs_of[0] for refs_of in local]

    def send(part, slot, buffer, place, sem, target):
        pltpu.make_async_remote_copy(
            src_ref=view(own, part, slot),
            dst_ref=view(buffer, part, place),
            send_sem=send_sem.at[part[1]],
            recv_sem=sem.at[part[0], place],
            device_id=target,
            device_id_type=MESH_IDS,
        ).start()

    def settle(part, slot, found):
        if len(found) > 1:
            add_up(found[0], found)

    def axes(part):
        if part[4] == 0:
            return here.y, here.x, y_count, x_count
        return here.x, here.y, x_count, y_count

    def place_of(part, a, b):
        return (a, b) if part[4] == 0 else (b, a)

    def cross_place(part, z, a_shift, b_shift, a_count, b_count):
        return ((z // 2) * (a_count - 1) + a_shift - 1) * (b_count - 1) + b_shift - 1

    def far_pairs(part, step):
        a_own, b_own, a_count, b_count = axes(part)
        repeat(a_count - 1, lambda i: repeat(b_count - 1, lambda j: step(1 + i, 1 + j)))

    def loop(count, step):
        lax.fori_loop(0, count, lambda i, carry: (step(i), carry)[1], 0)

    def plane_in_order(i):
        base = beside + (i // 2) * (here.z - beside)
        return (base + 2 * (1 - i % 2)) % PLANES

    def to_beside(part):
        a_own, b_own, a_count, b_count = axes(part)

        def one(z, a_shift, b_shift):
            y, x = place_of(part, (a_own + a_shift) % a_count, (b_own + b_shift) % b_count)
            slot = spot(z, y, x)
            settle(part, slot, terms_of(part, slot))
            place = cross_place(part, z, a_shift, b_shift, a_count, b_count)
            send(part, slot, cross, place, cross_sem, here.address(beside, here.y, here.x, here.core))

        loop(2, lambda i: far_pairs(part, lambda p, q: one(plane_in_order(i), p, q)))

    def to_second(part, z, a_shift, b_shift, crosses):
        a_own, b_own, a_count, b_count = axes(part)
        a, b = (a_own + a_shift) % a_count, (b_own + b_shift) % b_count
        y, x = place_of(part, a, b)
        slot = spot(z, y, x)
        found = terms_of(part, slot)
        if crosses:
            found.append(
                landed(cross, part, cross_place(part, z, a_shift, b_shift, a_count, b_count), cross_sem)
            )
        settle(part, slot, found)
        ty, tx = place_of(part, a_own, b)
        place = second_place(b_count - b_shift - 1, z, a_shift, a_count, b_count)
        send(part, slot, second, place, second_sem, here.address(here.z, ty, tx, here.core))

    def second_place(j, z, a_shift, a_count, b_count):
        if isinstance(a_shift, int) and a_shift == 0:
            return j * PLANES + z
        return (b_count - 1) * PLANES + (j * 2 + z // 2) * (a_count - 1) + a_shift - 1

    def from_second(part, z, a_shift):
        _, _, a_count, b_count = axes(part)
        return [
            landed(second, part, second_place(j, z, a_shift, a_count, b_count), second_sem)
            for j in range(b_count - 1)
        ]

    def to_first(part, z, a_shift, crosses):
        a_own, b_own, a_count, b_count = axes(part)
        a = (a_own + a_shift) % a_count
        y, x = place_of(part, a, b_own)
        slot = spot(z, y, x)
        found = terms_of(part, slot)
        if crosses:
            found += from_second(part, z, a_shift)
        settle(part, slot, found)
        place = (a_count - a_shift - 1) * PLANES + z
        send(part, slot, first, place, first_sem, here.address(here.z, y, x, here.core))

    def collect(part, z):
        a_own, b_own, a_count, b_count = axes(part)
        found = terms_of(part, spot(z, here.y, here.x)) + from_second(part, z, 0)
        return found + [landed(first, part, i * PLANES + z, first_sem) for i in range(a_count - 1)]

    def to_plane(part, z):
        slot = spot(z, here.y, here.x)
        settle(part, slot, collect(part, z))
        place = (here.z - z + PLANES) % PLANES - 1
        send(part, slot, planes, place, plane_sem, here.address(z, here.y, here.x, here.core))

    seen = set()
    for kind in (1, 0, 5, 3, 4, 2, 6):
        fetch_left(kind)

    def stage_fetch(parts):
        works, ready_kinds = backward.before(phases.index(parts)) if fused else ((), ())
        for work in works:
            work()
        for kind in ready_kinds:
            fetch_right(kind)
        for part in parts:
            if part[1] not in seen and part[1] not in ready_kinds and not (fused and part[1] != 1):
                fetch_right(part[1])
            seen.add(part[1])

    ready = set()

    def stage_terms(parts):
        for part in parts:
            if part[1] not in ready:
                fetched(part[1])
            ready.add(part[1])
            multiply(part)
            to_beside(part)

    def stage_out(parts):
        for part in parts:
            b_count = axes(part)[3]
            a_count = axes(part)[2]
            loop(
                4,
                lambda i: repeat(b_count - 1, lambda j: to_second(part, plane_in_order(i), 0, 1 + j, False)),
            )
            loop(2, lambda i: repeat(a_count - 1, lambda j: to_first(part, plane_in_order(i), 1 + j, False)))
            loop(2, lambda i: far_pairs(part, lambda p, q: to_second(part, plane_in_order(2 + i), p, q, True)))

    def stage_first(parts):
        for part in parts:
            a_count = axes(part)[2]
            loop(2, lambda i: repeat(a_count - 1, lambda j: to_first(part, plane_in_order(2 + i), 1 + j, True)))

    def stage_planes(parts):
        for part in parts:
            loop(3, lambda i: to_plane(part, plane_in_order((2 + i) % 3)))

    def stage_finish(parts):
        for part in parts:
            found = collect(part, here.z)
            found += [landed(planes, part, place, plane_sem) for place in range(PLANES - 1)]
            add_up_lines(sums[part[1]], shapes[part[1]], part[2], found)

    stages = (stage_fetch, stage_terms, stage_out, stage_first, stage_planes, stage_finish)
    for step in range(len(phases) + len(stages) - 1):
        for lag, stage in reversed(list(enumerate(stages))):
            if 0 <= step - lag < len(phases):
                stage(phases[step - lag])
    for kind in range(kinds):
        for copy in (theirs_left(kind) if direct[kind] else []) + theirs_right(kind):
            copy.wait_send()
        sent = own[kind].at[pl.ds(0, half - 1)]
        pltpu.make_async_copy(sent, sent, send_sem.at[kind]).wait()


def scatter_all(factors, shapes, wide, narrow, weights=(), streamed=(), given=()):
    devices = wide * narrow
    columns = wide // (PLANES * CORES)
    kinds = len(shapes)
    half = devices // CORES
    low = jnp.bfloat16
    direct, operands, scratch = [], [], []
    fused = bool(given)
    for kind, pair in enumerate(factors):
        rows, cols = shapes[kind]
        direct.append(len(pair) == 2 and rows % 16 == 0)
        if direct[kind]:
            left, right = pair
            operands.append(left.reshape(PLANES * columns, CORES, narrow * rows, left.shape[1]))
            if right is not None:
                operands.append(right)
        elif pair:
            terms = pair[0]
            if len(pair) == 2:
                terms = jnp.dot(pair[0], pair[1], preferred_element_type=jnp.float32).astype(low)
            terms = terms.reshape(PLANES * columns, CORES, narrow, rows, cols)
            operands.append(jnp.moveaxis(terms, 1, 0).reshape(CORES, half, rows, cols))
    orders = ((columns, narrow), (narrow, columns))
    counts = (
        half,
        max((b - 1) * (PLANES + 2 * (a - 1)) for a, b in orders),
        max((a - 1) * PLANES for a, b in orders),
        PLANES - 1,
        2 * (columns - 1) * (narrow - 1),
    )
    for stage in range(5):
        for kind in range(kinds):
            if stage == 0 and not direct[kind]:
                scratch.append(pltpu.VMEM((half,) + shapes[kind], low))
            else:
                scratch.append(pltpu.VMEM((counts[stage],) + shapes[kind], low))
    for kind in range(kinds):
        rows, cols = shapes[kind]
        if not direct[kind]:
            scratch.append(pltpu.VMEM((half, rows, cols), low))
            continue
        tokens = factors[kind][0].shape[1]
        depth = tokens if kind == SHARED else 2 * tokens
        scratch.append(pltpu.VMEM((PLANES * columns, narrow * rows, depth), low))
        scratch.append(pltpu.VMEM((depth, cols), low))
        if kind == SHARED:
            scratch.append(pltpu.VMEM((depth, cols), low))
    outs = []
    if fused:
        full = jnp.float32
        outs = [
            jax.ShapeDtypeStruct((PATCHES, D), low),
            jax.ShapeDtypeStruct((PATCH_PIXELS * VARS, PATCHES), full),
        ]
        rows_in, rows_out = shapes[0][0], shapes[1][0]
        scratch += [
            pltpu.VMEM((CORES, half) + shapes[6], low),
            pltpu.VMEM((2, TILE // rows_out, rows_out, D), low),
            pltpu.VMEM((2, TILE // rows_in, rows_in, FF), low),
            pltpu.VMEM((2, PATCHES, TILE), full),
            pltpu.VMEM((2, TILE, PATCHES), low),
            pltpu.VMEM((PATCHES, D), full),
            pltpu.VMEM((PATCHES, D), full),
            pltpu.VMEM((PATCHES, D), low),
            pltpu.VMEM((16, D), full),
            pltpu.VMEM((VARS * (PATCH_PIXELS + 1), LANES), full),
            pltpu.VMEM((D // LANES, PATCHES, LANES), full),
            pltpu.VMEM((devices * shapes[6][0], LANES), full),
            pltpu.SemaphoreType.DMA((2, 3)),
        ]
    widths = [s[1] for s in shapes]
    parts = sum(len(phase) for phase in phase_parts(widths, devices, SUM_PHASES, COARSE_SUM_PHASES))
    scratch += [pltpu.SemaphoreType.DMA((kinds,))] + [pltpu.SemaphoreType.DMA((kinds, 2))] * 3
    scratch += [pltpu.SemaphoreType.DMA((parts, counts[stage])) for stage in range(1, 5)]
    operands += list(weights) + list(streamed)
    found = pl.pallas_call(
        functools.partial(scatter_kernel, tuple(direct), tuple(shapes), wide, narrow, fused),
        out_shape=[jax.ShapeDtypeStruct((s[0] * s[1] // LANES, LANES), jnp.float32) for s in shapes] + outs,
        in_specs=[pl.BlockSpec(memory_space=pl.ANY)] * len(operands)
        + [pl.BlockSpec(memory_space=pltpu.VMEM)] * len(given),
        out_specs=[pl.BlockSpec(memory_space=pltpu.VMEM)] * (kinds + len(outs)),
        scratch_shapes=scratch,
        compiler_params=pltpu.CompilerParams(
            collective_id=1, has_side_effects=True, vmem_limit_bytes=VMEM_BYTES
        ),
        name="scatter_all",
    )(*operands, *given)
    return found[:kinds], found[kinds:]


def hand_over_kernel(*refs):
    for source, target in zip(refs[: len(refs) // 2], refs[len(refs) // 2 :]):
        target[...] = source[...]


def hand_over(arrays):
    return pl.pallas_call(
        hand_over_kernel,
        out_shape=[jax.ShapeDtypeStruct(a.shape, a.dtype) for a in arrays],
        in_specs=[pl.BlockSpec(memory_space=pltpu.VMEM)] * len(arrays),
        out_specs=[pl.BlockSpec(memory_space=pltpu.VMEM)] * len(arrays),
        name="hand_over",
    )(*arrays)


def small_size(shards):
    need = sum(s.size for s in shards)
    return -(-need // (16 * LANES)) * 16 * LANES


def on_device(
    fields,
    var_ids,
    slot_mask,
    embed_table,
    agg_in,
    agg_out,
    attn_in,
    attn_out,
    mlp_in,
    mlp_out,
    vectors,
    positions,
    cotangent,
):
    wide, narrow = lax.axis_size("wide"), lax.axis_size("narrow")
    devices = wide * narrow
    small = (embed_table, vectors, positions)
    pad = small_size(small) - sum(s.size for s in small)
    small_block = jnp.concatenate(small + (jnp.zeros((pad,), embed_table.dtype),))
    head_size = D // HEADS
    score_scale = head_size ** (-0.5)
    length = PATCHES
    single_float = jnp.float32
    bf16 = jnp.bfloat16
    fused = fits(devices)
    order = jnp.array(variable_order(devices)) if fused else jnp.arange(VARS)
    onehot = (var_ids[0][:, None] == order[None, :]).astype(bf16)
    var_pixels = jnp.einsum("sv,spl->pvl", onehot, fields[0], preferred_element_type=single_float)
    live = jnp.einsum("sv,s->v", onehot, slot_mask[0].astype(bf16), preferred_element_type=single_float)
    pixels = jnp.concatenate([var_pixels, jnp.ones((1, VARS, length), single_float)], 0)
    given = ()
    if fused:
        given = (pixels.reshape(-1, length), jnp.broadcast_to(live[:, None], (VARS, length)))
    gathered, found = gather_all(
        (
            mlp_in,
            mlp_out,
            agg_in,
            attn_in,
            agg_out,
            attn_out,
            small_block,
        ),
        (FF, D, 3 * D, 3 * D, D, D, LANES),
        wide,
        narrow,
        given,
    )
    mlp_in_full = gathered[0].reshape(D, FF)
    mlp_out_full = gathered[1].reshape(FF, D)
    agg_in_full = gathered[2].reshape(D, 3 * D)
    attn_in_full = gathered[3].reshape(D, 3 * D)
    agg_out_full = gathered[4].reshape(D, D)
    attn_out_full = gathered[5].reshape(D, D)
    cut_one = embed_table.size
    cut_two = cut_one + vectors.size
    cut_three = cut_two + positions.size
    shapes = tuple(
        (count // (cols * devices), cols)
        for count, cols in (
            (D * FF, FF),
            (FF * D, D),
            (3 * D * D, 3 * D),
            (3 * D * D, 3 * D),
            (D * D, D),
            (D * D, D),
            (small_block.size * devices, LANES),
        )
    )
    if fused:
        (
            table_left,
            row_values,
            table_keys,
            table_values,
            key_dots,
            agg_probs,
            mixture_left,
            stream,
            normed1_left,
            projected,
            self_probs,
            attended_left,
            stream1,
            normed2_left,
            hidden,
            activated_left,
        ) = found
        summed, (result, grad_pixels) = scatter_all(
            (
                (normed2_left, None),
                (activated_left, cotangent[0]),
                (table_left, None),
                (normed1_left, None),
                (mixture_left, None),
                (attended_left, None),
                (),
            ),
            shapes,
            wide,
            narrow,
            gathered[:6],
            (hidden, activated_left),
            (
                row_values,
                table_keys,
                table_values,
                key_dots,
                agg_probs,
                stream,
                projected,
                self_probs,
                stream1,
                given[0],
                cotangent[0],
            ),
        )
        grad_pixels = grad_pixels.reshape(PATCH_PIXELS, VARS, length).astype(bf16)
        fields_grad = jnp.einsum(
            "sv,pvl->spl", onehot, grad_pixels, preferred_element_type=single_float
        ).astype(bf16)
    else:
        small_rows = gathered[6].reshape(devices, -1)
        table_full = small_rows[:, :cut_one].reshape(VARS, (PATCH_PIXELS + 1) * D)
        vector_rows = small_rows[:, cut_one:cut_two].reshape(VEC_ROWS, D)
        position_rows = small_rows[:, cut_two:cut_three].reshape(PATCHES, D)
        table_rows = table_full.reshape(VARS, PATCH_PIXELS + 1, D).transpose(1, 0, 2).reshape(-1, D)
        query_row = vector_rows[0]
        agg_query = jnp.dot(
            query_row[None, :], agg_in_full[:, :D], preferred_element_type=single_float
        )[0].astype(bf16)
        table_kv = jnp.dot(table_rows, agg_in_full[:, D:], preferred_element_type=single_float)
        table_keys = table_kv[:, :D]
        table_values = table_kv[:, D:].astype(bf16).reshape(-1, HEADS, head_size)
        query_wide = agg_query.astype(single_float)
        key_dots = (
            jnp.sum((table_keys * query_wide).reshape(-1, HEADS, head_size), -1) * score_scale
        ).reshape(PATCH_PIXELS + 1, VARS, HEADS).transpose(0, 2, 1)
        agg_scores = jnp.sum(pixels[:, None] * key_dots[..., None], 0)
        agg_scores = jnp.where(live[None, :, None] > 0, agg_scores, masked_score)
        score_top = jnp.max(agg_scores, 1, keepdims=True)
        agg_expo = jnp.exp(agg_scores - score_top)
        agg_probs = agg_expo / jnp.sum(agg_expo, 1, keepdims=True)
        spread = (agg_probs[:, None] * pixels[None]).astype(bf16).reshape(HEADS, -1, length)
        mixture = (
            jnp.einsum("hrl,rhc->lhc", spread, table_values, preferred_element_type=single_float)
            .reshape(length, D)
            .astype(bf16)
        )
        row_values = vector_rows.astype(single_float)
        position_values = position_rows.astype(single_float)
        stream = jnp.dot(mixture, agg_out_full, preferred_element_type=single_float) + position_values
        normed1 = layer_norm(stream, row_values[1], row_values[2]).astype(bf16)
        qkv_bias = jnp.concatenate([row_values[3], jnp.zeros((2 * D,), single_float)])
        projected = (
            jnp.dot(normed1, attn_in_full, preferred_element_type=single_float) + qkv_bias
        ).astype(bf16)
        queries = projected[:, :D].reshape(length, HEADS, head_size)
        keys = projected[:, D : 2 * D].reshape(length, HEADS, head_size)
        values = projected[:, 2 * D :].reshape(length, HEADS, head_size)
        self_scores = (
            jnp.einsum("ihc,jhc->hij", queries, keys, preferred_element_type=single_float) * score_scale
        )
        score_peak = jnp.max(self_scores, -1, keepdims=True)
        self_lse = score_peak + jnp.log(jnp.sum(jnp.exp(self_scores - score_peak), -1, keepdims=True))
        self_probs = jnp.exp(self_scores - self_lse)
        probs_low = self_probs.astype(bf16)
        attended = (
            jnp.einsum("hij,jhc->ihc", probs_low, values, preferred_element_type=single_float)
            .reshape(length, D)
            .astype(bf16)
        )
        stream1 = (
            stream
            + jnp.dot(attended, attn_out_full, preferred_element_type=single_float)
            + row_values[4]
        )
        normed2 = layer_norm(stream1, row_values[5], row_values[6]).astype(bf16)
        hidden = jnp.dot(normed2, mlp_in_full, preferred_element_type=single_float) + row_values[
            8:VEC_ROWS
        ].reshape(FF)
        activated = gelu_exact(hidden).astype(bf16)
        queries = projected[:, :D].reshape(length, HEADS, head_size)
        keys = projected[:, D : 2 * D].reshape(length, HEADS, head_size)
        values = projected[:, 2 * D :].reshape(length, HEADS, head_size)
        result = (
            stream1
            + jnp.dot(activated, mlp_out_full, preferred_element_type=single_float)
            + row_values[7]
        ).astype(bf16)
        grad_output = cotangent[0].astype(single_float)
        grad_branch2 = grad_output.astype(bf16)
        grad_fc2_bias = jnp.sum(grad_branch2.astype(single_float), 0)
        grad_activated = jnp.dot(grad_branch2, mlp_out_full.T, preferred_element_type=single_float)
        gelu_value, gelu_pull = jax.vjp(gelu_exact, hidden)
        grad_hidden = gelu_pull(grad_activated)[0].astype(bf16)
        grad_fc1_bias = jnp.sum(grad_hidden.astype(single_float), 0)
        grad_normed2 = jnp.dot(grad_hidden, mlp_in_full.T, preferred_element_type=single_float)
        norm_value2, norm2_pull = jax.vjp(layer_norm, stream1, row_values[5], row_values[6])
        back_stream1, grad_gain2, grad_shift2 = norm2_pull(grad_normed2)
        grad_stream1 = grad_output + back_stream1
        grad_branch1 = grad_stream1.astype(bf16)
        grad_proj_bias = jnp.sum(grad_branch1.astype(single_float), 0)
        grad_attended = (
            jnp.dot(grad_branch1, attn_out_full.T, preferred_element_type=single_float)
            .astype(bf16)
            .reshape(length, HEADS, head_size)
        )
        again_probs = self_probs
        again_low = again_probs.astype(bf16)
        grad_probs = jnp.einsum(
            "ihc,jhc->hij", grad_attended, values, preferred_element_type=single_float
        )
        grad_self_scores = (
            again_probs * (grad_probs - jnp.sum(again_probs * grad_probs, -1, keepdims=True))
        ).astype(bf16)
        grad_queries = (
            jnp.einsum("hij,jhc->ihc", grad_self_scores, keys, preferred_element_type=single_float)
            * score_scale
        )
        grad_keys = (
            jnp.einsum("hij,ihc->jhc", grad_self_scores, queries, preferred_element_type=single_float)
            * score_scale
        )
        grad_values = jnp.einsum(
            "hij,ihc->jhc", again_low, grad_attended, preferred_element_type=single_float
        )
        grad_projected = jnp.concatenate(
            [
                grad_queries.reshape(length, D),
                grad_keys.reshape(length, D),
                grad_values.reshape(length, D),
            ],
            1,
        ).astype(bf16)
        grad_query_bias = jnp.sum(grad_projected[:, :D].astype(single_float), 0)
        grad_normed1 = jnp.dot(grad_projected, attn_in_full.T, preferred_element_type=single_float)
        norm_value1, norm1_pull = jax.vjp(layer_norm, stream, row_values[1], row_values[2])
        back_stream, grad_gain1, grad_shift1 = norm1_pull(grad_normed1)
        grad_stream = grad_stream1 + back_stream
        grad_agg_branch = grad_stream.astype(bf16)
        grad_mixture = (
            jnp.dot(grad_agg_branch, agg_out_full.T, preferred_element_type=single_float)
            .astype(bf16)
            .reshape(length, HEADS, head_size)
        )
        back_mix = jnp.einsum(
            "rhc,lhc->hrl", table_values, grad_mixture, preferred_element_type=single_float
        ).reshape(HEADS, PATCH_PIXELS + 1, VARS, length)
        grad_agg_probs = jnp.sum(back_mix * pixels[None], 1)
        grad_agg_scores = agg_probs * (
            grad_agg_probs - jnp.sum(agg_probs * grad_agg_probs, 1, keepdims=True)
        )
        grad_pixels = jnp.sum(
            grad_agg_scores[:, None] * key_dots.transpose(1, 0, 2)[..., None]
            + agg_probs[:, None] * back_mix,
            0,
        )[:PATCH_PIXELS].astype(bf16)
        fields_grad = jnp.einsum(
            "sv,pvl->spl", onehot, grad_pixels, preferred_element_type=single_float
        ).astype(bf16)
        grad_dots = (
            jnp.sum(pixels[None] * grad_agg_scores[:, None], -1) * score_scale
        ).reshape(HEADS, -1).T
        grad_table_values = jnp.einsum(
            "hrl,lhc->rhc", spread, grad_mixture, preferred_element_type=single_float
        ).reshape(-1, D)
        dots_wide = jnp.repeat(grad_dots, head_size, 1)
        grad_agg_query = jnp.sum(dots_wide * table_keys, 0)
        grad_table_kv = jnp.concatenate([dots_wide * query_wide, grad_table_values], 1).astype(bf16)
        grad_table = (
            jnp.dot(grad_table_kv, agg_in_full[:, D:].T, preferred_element_type=single_float)
            .reshape(PATCH_PIXELS + 1, VARS, D)
            .transpose(1, 0, 2)
        )
        filling = 2 * LANES - table_rows.shape[0] - 1
        table_and_query = jnp.concatenate([table_rows, query_row[None, :], jnp.zeros((filling, D), bf16)], 0)
        grad_table_and_query = jnp.concatenate(
            [
                jnp.pad(grad_table_kv, ((0, 0), (D, 0))),
                jnp.pad(grad_agg_query.astype(bf16)[None, :], ((0, 0), (0, 2 * D))),
                jnp.zeros((filling, 3 * D), bf16),
            ],
            0,
        )
        grad_query_row = jnp.dot(
            agg_in_full[:, :D].astype(single_float), grad_agg_query, precision=highest_precision
        )
        grad_rows = jnp.concatenate(
            [
                jnp.stack(
                    [
                        grad_query_row,
                        grad_gain1,
                        grad_shift1,
                        grad_query_bias,
                        grad_proj_bias,
                        grad_gain2,
                        grad_shift2,
                        grad_fc2_bias,
                    ]
                ),
                grad_fc1_bias.reshape(FF // D, D),
            ],
            0,
        )
        small_terms = jnp.concatenate(
            [
                grad_table.astype(bf16).reshape(devices, -1),
                grad_rows.astype(bf16).reshape(devices, -1),
                grad_stream.astype(bf16).reshape(devices, -1),
                jnp.zeros((devices, pad), bf16),
            ],
            1,
        ).reshape(devices, -1, LANES)
        summed, _ = scatter_all(
            (
                (normed2.T, grad_hidden),
                (activated.T, grad_branch2),
                (table_and_query.T, grad_table_and_query),
                (normed1.T, grad_projected),
                (mixture.T, grad_agg_branch),
                (attended.T, grad_branch1),
                (small_terms,),
            ),
            shapes,
            wide,
            narrow,
        )
    if fused:
        summed = hand_over(summed)
    flat_small = summed[6].reshape(-1)
    return (
        result[None],
        fields_grad[None],
        flat_small[:cut_one],
        summed[2].reshape(-1),
        summed[4].reshape(-1),
        summed[3].reshape(-1),
        summed[5].reshape(-1),
        summed[0].reshape(-1),
        summed[1].reshape(-1),
        flat_small[cut_one:cut_two],
        flat_small[cut_two:cut_three],
    )


def solution(mesh):
    return jax.shard_map(
        on_device,
        mesh=mesh,
        in_specs=(
            P(("wide", "narrow"), None, None, None),
            P(("wide", "narrow"), None),
            P(("wide", "narrow"), None),
            P(("wide", "narrow")),
            P(("wide", "narrow")),
            P(("wide", "narrow")),
            P(("wide", "narrow")),
            P(("wide", "narrow")),
            P(("wide", "narrow")),
            P(("wide", "narrow")),
            P(("wide", "narrow")),
            P(("wide", "narrow")),
            P(("wide", "narrow"), None, None),
        ),
        out_specs=(
            P(("wide", "narrow"), None, None),
            P(("wide", "narrow"), None, None, None),
            P(("wide", "narrow")),
            P(("wide", "narrow")),
            P(("wide", "narrow")),
            P(("wide", "narrow")),
            P(("wide", "narrow")),
            P(("wide", "narrow")),
            P(("wide", "narrow")),
            P(("wide", "narrow")),
            P(("wide", "narrow")),
        ),
        check_vma=False,
    )
```

profile of v0, /device:TPU:8, one launch (start us, length us, event | category | flops | bytes accessed | tf_op | source)
XLA Modules:
  0.0 344.6 jit_solution(12230301813305877932)
XLA Ops:
  0.6 0.0 copy-start
  0.7 0.8 copy-done
  1.4 0.9 convolution_bitcast_fusion.1
  2.3 1.4 maximum_bitcast_fusion.refs_6_
  3.7 0.7 broadcast_in_dim.18.refs_8_
  4.4 0.9 convolution_bitcast_fusion
  5.3 0.7 concatenate.7
  6.0 155.8 %gather_all.1 = (bf16[32,32,4096]{2,1,0:T(8,128)(2,1)}, bf16[32,128,1024]{2,1,0:T(8,128)(2,1)}, bf16[32,32,3072]{2,1,0:T(8,128)(2,1)}, bf16[32,32,3072]{2,1,0:T(...) custom-call(bf16[1024,128]{1,0:T(8,128)(2,1)} %bitcast.59, ...), custom_call_target="tpu_custom_call" | custom-call | tf_op jit(solution)/shard_map/gather_all/pallas_call | solution.py:976
  161.8 0.0 copy-start.1
  161.8 0.0 copy-start.2
  161.8 172.5 %scatter_all.1 = (f32[1024,128]{1,0:T(8,128)}, f32[1024,128]{1,0:T(8,128)}, f32[768,128]{1,0:T(8,128)}, f32[768,128]{1,0:T(8,128)}, f32[256,128]{1,0:T(8,128)}, ...) custom-call(bf16[8,2,64,128]{3,2,1,0:T(8,128)(2,1)} %bitcast.58, ...), custom_call_target="tpu_custom_call" | custom-call | tf_op jit(solution)/shard_map/scatter_all/pallas_call | solution.py:1423
  334.3 0.9 convert_element_type.18
  335.2 0.0 copy-done.1
  335.2 0.0 copy-done.2
  335.3 0.2 fusion
  335.5 0.6 copy.27
  336.1 2.8 hand_over.1
  338.9 1.3 slice_bitcast_fusion.2
  340.2 1.3 slice_bitcast_fusion.1
  341.5 1.4 slice_bitcast_fusion
  342.9 1.7 copy.33
  (1 shorter events, 0.0 us)
Async XLA Ops:
  0.6 0.8 copy-start
  161.8 173.4 %copy-start.1 = (s32[1,48]{1,0:T(1,128)S(1)}, s32[1,48]{1,0:T(1,128)}, u32[]{:S(2)}) copy-start(s32[1,48]{1,0:T(1,128)} %param.15) | copy-start | bytes 580
  161.8 173.4 %copy-start.2 = (s32[48]{0:T(128)S(1)}, s32[48]{0:T(128)}, u32[]{:S(2)}) copy-start(s32[48]{0:T(128)} %constant.6.clone) | copy-start | bytes 580
where the time goes:
time: 348 us; the launch traced here: 345 us
  Pallas kernels  331 us (95%)
  local copies, waits for them, and re-layouts  8.43 us (2%)
    pallas_call x1, Pallas kernels, scatter_all(): pl.pallas_call(functools.partial(scatter_kernel, tuple(direct), tuple(sha...  172 us
    pallas_call x1, Pallas kernels, gather_all(): pl.pallas_call(functools.partial(gather_kernel, widths, wide, narrow, fus...  156 us

commit v1 on v0

--- a/solution.py
+++ b/solution.py
@@ -22,7 +22,7 @@
 TILE = 256
 SHARED = 2
 MESH_IDS = pl.DeviceIdType.MESH
-VMEM_BYTES = 66 * 1000 * 1000
+VMEM_BYTES = 67 * 1000 * 1000
 
 
 norm_eps = 1e-05
@@ -153,8 +153,28 @@
     )
 
 
-class Forward:
+class Work:
+    def __init__(self):
+        self.chunks = []
+
+    def do(self, chunk):
+        self.chunks.append(chunk)
+
+    def loop(self, count, step, pieces=1):
+        def one(first, last):
+            lax.fori_loop(first, last, lambda i, carry: (step(i), carry)[1], 0)
+
+        for piece in range(pieces):
+            self.do(functools.partial(one, count * piece // pieces, count * (piece + 1) // pieces))
+
+    def run(self, count):
+        for _ in range(min(count, len(self.chunks))):
+            self.chunks.pop(0)()
+
+
+class Forward(Work):
     def __init__(self, devices, weights, small, given, outs, scratch):
+        super().__init__()
         self.devices, self.weights, self.small = devices, weights, small
         self.pixels, self.live = given
         (
@@ -192,9 +212,6 @@
         count, rows, _ = weight.shape
         return weight[:, :, pl.ds(column, TILE)].reshape(count * rows, TILE)
 
-    def loop(self, count, step):
-        lax.fori_loop(0, count, lambda i, carry: (step(i), carry)[1], 0)
-
     def turn(self, source, target):
         def one(i):
             at = pl.multiple_of(i * TILE, TILE)
@@ -213,7 +230,8 @@
         per_row = D // LANES
         each, span, period = lines_of_variables(devices)
         count = VARS // period
-        for p in range(PATCH_PIXELS + 1):
+
+        def table_rows(p):
             for b in range(period):
                 for c in range(per_row):
                     line = ((PATCH_PIXELS + 1) * b + p) * per_row + c
@@ -221,24 +239,34 @@
                     self.table[pl.ds(p * VARS + b * count, count), pl.ds(c * LANES, LANES)] = self.lines[
                         pl.ds(start, count, stride=tall * span), :
                     ].astype(jnp.bfloat16)
-        first, each = each, VEC_ROWS * per_row // devices
-        for row in range(VEC_ROWS):
-            for c in range(per_row):
-                line = row * per_row + c
-                start = tall * (line // each) + first + line % each
-                self.rows[pl.ds(row, 1), pl.ds(c * LANES, LANES)] = self.lines[pl.ds(start, 1), :]
-        first, rows = first + each, PATCHES // devices
-        for row in range(rows):
-            for c in range(per_row):
-                start = first + row * per_row + c
-                self.positions[c, pl.ds(row, devices, stride=rows), :] = self.lines[
-                    pl.ds(start, devices, stride=tall), :
-                ]
+
+        for p in range(PATCH_PIXELS + 1):
+            self.do(functools.partial(table_rows, p))
+        of_vectors = VEC_ROWS * per_row // devices
+
+        def vectors():
+            for row in range(VEC_ROWS):
+                for c in range(per_row):
+                    line = row * per_row + c
+                    start = tall * (line // of_vectors) + each + line % of_vectors
+                    self.rows[pl.ds(row, 1), pl.ds(c * LANES, LANES)] = self.lines[pl.ds(start, 1), :]
+
+        self.do(vectors)
+        first, rows = each + of_vectors, PATCHES // devices
+
+        def positions():
+            for row in range(rows):
+                for c in range(per_row):
+                    start = first + row * per_row + c
+                    self.positions[c, pl.ds(row, devices, stride=rows), :] = self.lines[
+                        pl.ds(start, devices, stride=tall), :
+                    ]
+
+        self.do(positions)
 
     def table_products(self):
-        head = self.rows[0:8, :].astype(jnp.bfloat16)
-
         def query(i):
+            head = self.rows[0:8, :].astype(jnp.bfloat16)
             column = pl.multiple_of(i * TILE, TILE)
             found = mul(head, self.tile(2, column)).astype(jnp.bfloat16).astype(jnp.float32)
             self.query[:, pl.ds(column, TILE)] = found
@@ -255,20 +283,25 @@
             )
 
         self.loop(D // TILE, query)
-        self.loop(D // TILE, key)
-        self.loop(D // TILE, value)
-        size = D // HEADS
-        unit = lax.broadcasted_iota(jnp.int32, (D, LANES), 0)
-        head_first = lax.broadcasted_iota(jnp.int32, (D, LANES), 1) * size
-        member = jnp.where((unit >= head_first) & (unit < head_first + size), 1.0, 0.0)
-        self.dots[...] = mul(self.keys[...] * self.query[0:1, :], member, precision=highest_precision) * size**-0.5
+        self.loop(D // TILE, key, 2)
+        self.loop(D // TILE, value, 2)
+
+        def dots():
+            size = D // HEADS
+            unit = lax.broadcasted_iota(jnp.int32, (D, LANES), 0)
+            head_first = lax.broadcasted_iota(jnp.int32, (D, LANES), 1) * size
+            member = jnp.where((unit >= head_first) & (unit < head_first + size), 1.0, 0.0)
+            found = mul(self.keys[...] * self.query[0:1, :], member, precision=highest_precision)
+            self.dots[...] = found * size**-0.5
+
+        self.do(dots)
 
     def aggregate(self):
         size = D // HEADS
-        lane = lax.broadcasted_iota(jnp.int32, self.dots.shape, 1)
-        low_half = lax.broadcasted_iota(jnp.int32, (PATCHES, LANES), 1) < size
 
         def pair(g):
+            lane = lax.broadcasted_iota(jnp.int32, self.dots.shape, 1)
+            low_half = lax.broadcasted_iota(jnp.int32, (PATCHES, LANES), 1) < size
             columns = pl.ds(pl.multiple_of(g * LANES, LANES), LANES)
             halves = []
             for i in range(2):
@@ -288,17 +321,21 @@
                 halves.append(mul(self.spread[h], self.values[:, columns], ((0,), (0,))))
             self.mixture[:, columns] = jnp.where(low_half, halves[0], halves[1]).astype(jnp.bfloat16)
 
-        self.loop(HEADS // 2, pair)
+        self.loop(HEADS // 2, pair, 4)
         self.turn(self.mixture, self.mixture_left)
-        table = self.table.shape[0]
-        filling = self.table_left.shape[1] - table
-        first = lax.broadcasted_iota(jnp.int32, (filling, LANES), 0) == 0
-        for c in range(D // LANES):
-            columns = slice(c * LANES, (c + 1) * LANES)
-            block = jnp.concatenate(
-                [self.table[:, columns].astype(jnp.float32), jnp.where(first, self.rows[0:1, columns], 0.0)], 0
-            )
-            self.table_left[columns, :] = block.T.astype(jnp.bfloat16)
+
+        def table_left():
+            table = self.table.shape[0]
+            filling = self.table_left.shape[1] - table
+            first = lax.broadcasted_iota(jnp.int32, (filling, LANES), 0) == 0
+            for c in range(D // LANES):
+                columns = slice(c * LANES, (c + 1) * LANES)
+                block = jnp.concatenate(
+                    [self.table[:, columns].astype(jnp.float32), jnp.where(first, self.rows[0:1, columns], 0.0)], 0
+                )
+                self.table_left[columns, :] = block.T.astype(jnp.bfloat16)
+
+        self.do(table_left)
 
     def join(self):
         def one(i):
@@ -307,7 +344,12 @@
             self.stream[:, columns] = mul(self.mixture[...], self.tile(4, pl.multiple_of(i * TILE, TILE))) + shift
 
         self.loop(D // TILE, one)
-        self.normed1[...] = layer_norm(self.stream[...], self.rows[1:2, :], self.rows[2:3, :]).astype(jnp.bfloat16)
+
+        def norm():
+            found = layer_norm(self.stream[...], self.rows[1:2, :], self.rows[2:3, :])
+            self.normed1[...] = found.astype(jnp.bfloat16)
+
+        self.do(norm)
         self.turn(self.normed1, self.normed1_left)
 
     def project(self):
@@ -321,14 +363,14 @@
             column = pl.multiple_of(D + i * TILE, TILE)
             self.projected[:, pl.ds(column, TILE)] = mul(self.normed1[...], self.tile(3, column)).astype(jnp.bfloat16)
 
-        self.loop(D // TILE, with_bias)
-        self.loop(2 * D // TILE, plain)
+        self.loop(D // TILE, with_bias, 2)
+        self.loop(2 * D // TILE, plain, 4)
 
     def attend(self):
         size = D // HEADS
-        low_half = lax.broadcasted_iota(jnp.int32, (PATCHES, LANES), 1) < size
 
         def pair(g):
+            low_half = lax.broadcasted_iota(jnp.int32, (PATCHES, LANES), 1) < size
             column = pl.multiple_of(g * LANES, LANES)
             queries, keys, values = (self.projected[:, pl.ds(third * D + column, LANES)] for third in range(3))
             halves = []
@@ -342,7 +384,7 @@
                 halves.append(mul(probs.astype(jnp.bfloat16), values))
             self.attended[:, pl.ds(column, LANES)] = jnp.where(low_half, halves[0], halves[1]).astype(jnp.bfloat16)
 
-        self.loop(HEADS // 2, pair)
+        self.loop(HEADS // 2, pair, 4)
 
     def join_attended(self):
         def one(i):
@@ -351,7 +393,12 @@
             self.stream1[:, columns] = found + self.rows[4:5, columns]
 
         self.loop(D // TILE, one)
-        self.normed2[...] = layer_norm(self.stream1[...], self.rows[5:6, :], self.rows[6:7, :]).astype(jnp.bfloat16)
+
+        def norm():
+            found = layer_norm(self.stream1[...], self.rows[5:6, :], self.rows[6:7, :])
+            self.normed2[...] = found.astype(jnp.bfloat16)
+
+        self.do(norm)
         self.turn(self.attended, self.attended_left)
         self.turn(self.normed2, self.normed2_left)
 
@@ -366,7 +413,7 @@
             self.hidden[:, columns] = found
             self.activated_left[columns, :] = gelu_exact(found).T.astype(jnp.bfloat16)
 
-        self.loop(FF // TILE, one)
+        self.loop(FF // TILE, one, 4)
 
     def after(self, phase):
         return {
@@ -386,8 +433,9 @@
     return down, jnp.sum(grad * unit, 0, keepdims=True), jnp.sum(grad, 0, keepdims=True)
 
 
-class Backward:
+class Backward(Work):
     def __init__(self, devices, narrow, weights, streamed, given, outs, rights, scratch):
+        super().__init__()
         self.devices, self.narrow, self.weights, self.rights = devices, narrow, weights, rights
         self.hidden, self.activated = streamed
         (
@@ -417,40 +465,32 @@
             self.grad_dots,
             self.positions,
             self.lines,
+            self.table_grad,
             self.tile_sem,
         ) = scratch
 
-    def loop(self, count, step):
-        lax.fori_loop(0, count, lambda i, carry: (step(i), carry)[1], 0)
-
-    def rolling(self, count, copies, step, unrolled=False):
-        for copy in copies(0, 0):
-            copy.start()
+    def rolling(self, count, copies, step, pieces=1):
+        def start():
+            for copy in copies(0, 0):
+                copy.start()
+
+        self.do(start)
 
         def one(i):
             slot = i % 2
-            if unrolled:
-                following = copies(i + 1, 1 - slot) if i + 1 < count else []
-                for copy in following:
+
+            def ahead():
+                for copy in copies(i + 1, 1 - slot):
                     copy.start()
-            else:
-
-                def ahead():
-                    for copy in copies(i + 1, 1 - slot):
-                        copy.start()
-
-                pl.when(i + 1 < count)(ahead)
+
+            pl.when(i + 1 < count)(ahead)
             for copy in copies(i, slot):
                 copy.wait()
             step(i, slot)
 
-        if unrolled:
-            for i in range(count):
-                one(i)
-        else:
-            self.loop(count, one)
-
-    def row_tiles(self, kind, step, unrolled=False):
+        self.loop(count, one, pieces)
+
+    def row_tiles(self, kind, step, pieces=1):
         weight = self.weights[kind]
         _, rows, cols = weight.shape
         blocks = TILE // rows
@@ -460,19 +500,19 @@
             return [pltpu.make_async_copy(weight.at[pl.ds(i * blocks, blocks)], target, self.tile_sem.at[slot, 0])]
 
         def one(i, slot):
-            column = i * TILE if unrolled else pl.multiple_of(i * TILE, TILE)
+            column = pl.multiple_of(i * TILE, TILE)
             step(column, lambda at, width: self.flat_tiles[slot, :, :, pl.ds(at, width)].reshape(TILE, width))
 
-        self.rolling(D // TILE, copies, one, unrolled)
-
-    def through(self, kind, left, target):
+        self.rolling(D // TILE, copies, one, pieces)
+
+    def through(self, kind, left, target, pieces=1):
         cols = self.weights[kind].shape[2]
 
         def one(column, weight):
             found = mul(left[...], weight(0, cols), ((1,), (1,)))
             target[:, pl.ds(column, TILE)] = found.astype(target.dtype)
 
-        self.row_tiles(kind, one)
+        self.row_tiles(kind, one, pieces)
 
     def right(self, kind):
         return self.rights[kind].at[pl.ds(0, PATCHES)]
@@ -497,7 +537,13 @@
                 ),
             ]
 
-        self.down[...] = self.stream1[...] + self.rows[7:8, :]
+        def base():
+            self.down[...] = self.stream1[...] + self.rows[7:8, :]
+
+        def finish():
+            self.result[...] = self.down[...].astype(jnp.bfloat16)
+
+        self.do(base)
 
         def one(i, slot):
             rows = self.tall_tiles[slot].reshape(TILE, D)
@@ -511,30 +557,34 @@
             there = pl.ds(pl.multiple_of((i % per_row) * TILE, TILE), TILE)
             self.grad_rows[pl.ds(8 + i // per_row, 1), there] = jnp.sum(grad.astype(jnp.float32), 0, keepdims=True)
 
-        self.rolling(FF // TILE, copies, one)
-        self.result[...] = self.down[...].astype(jnp.bfloat16)
+        self.rolling(FF // TILE, copies, one, 8)
+        self.do(finish)
 
     def norm2(self):
-        self.through(0, self.right(0), self.down)
-        grad = self.cotangent[...].astype(jnp.float32)
-        back, gain, shift = norm_back(self.stream1[...], self.down[...], self.rows[5:6, :])
-        self.grad_rows[5:6, :] = gain
-        self.grad_rows[6:7, :] = shift
-        self.grad_rows[7:8, :] = jnp.sum(grad, 0, keepdims=True)
-        total = grad + back
-        self.grad_stream1[...] = total
-        branch = total.astype(jnp.bfloat16)
-        self.right(5)[...] = branch
-        self.grad_rows[4:5, :] = jnp.sum(branch.astype(jnp.float32), 0, keepdims=True)
+        self.through(0, self.right(0), self.down, 2)
+
+        def norm():
+            grad = self.cotangent[...].astype(jnp.float32)
+            back, gain, shift = norm_back(self.stream1[...], self.down[...], self.rows[5:6, :])
+            self.grad_rows[5:6, :] = gain
+            self.grad_rows[6:7, :] = shift
+            self.grad_rows[7:8, :] = jnp.sum(grad, 0, keepdims=True)
+            total = grad + back
+            self.grad_stream1[...] = total
+            branch = total.astype(jnp.bfloat16)
+            self.right(5)[...] = branch
+            self.grad_rows[4:5, :] = jnp.sum(branch.astype(jnp.float32), 0, keepdims=True)
+
+        self.do(norm)
 
     def attend(self):
         self.through(5, self.right(5), self.narrow_grad)
         size = D // HEADS
         scale = size**-0.5
-        low_half = lax.broadcasted_iota(jnp.int32, (PATCHES, LANES), 1) < size
         grad_projected = self.right(3)
 
         def pair(g):
+            low_half = lax.broadcasted_iota(jnp.int32, (PATCHES, LANES), 1) < size
             column = pl.multiple_of(g * LANES, LANES)
             queries, keys, values = (self.projected[:, pl.ds(third * D + column, LANES)] for third in range(3))
             grad = self.narrow_grad[:, pl.ds(column, LANES)]
@@ -556,33 +606,45 @@
                 found = jnp.where(low_half, halves[0][third], halves[1][third])
                 grad_projected[:, pl.ds(third * D + column, LANES)] = found.astype(jnp.bfloat16)
 
-        self.loop(HEADS // 2, pair)
-        self.grad_rows[3:4, :] = jnp.sum(grad_projected[:, pl.ds(0, D)].astype(jnp.float32), 0, keepdims=True)
+        self.loop(HEADS // 2, pair, 4)
+
+        def bias():
+            self.grad_rows[3:4, :] = jnp.sum(grad_projected[:, pl.ds(0, D)].astype(jnp.float32), 0, keepdims=True)
+
+        self.do(bias)
 
     def norm1(self):
-        self.through(3, self.right(3), self.down)
-        back, gain, shift = norm_back(self.stream[...], self.down[...], self.rows[1:2, :])
-        self.grad_rows[1:2, :] = gain
-        self.grad_rows[2:3, :] = shift
-        total = self.grad_stream1[...] + back
-        self.right(4)[...] = total.astype(jnp.bfloat16)
-        for c in range(D // LANES):
-            self.positions[c] = total[:, c * LANES : (c + 1) * LANES]
+        self.through(3, self.right(3), self.down, 2)
+
+        def norm():
+            back, gain, shift = norm_back(self.stream[...], self.down[...], self.rows[1:2, :])
+            self.grad_rows[1:2, :] = gain
+            self.grad_rows[2:3, :] = shift
+            total = self.grad_stream1[...] + back
+            self.right(4)[...] = total.astype(jnp.bfloat16)
+            for c in range(D // LANES):
+                self.positions[c] = total[:, c * LANES : (c + 1) * LANES]
+
+        self.do(norm)
 
     def aggregate(self):
         self.through(4, self.right(4), self.narrow_grad)
         size = D // HEADS
         scale = size**-0.5
         table = VARS * (PATCH_PIXELS + 1)
-        lane = lax.broadcasted_iota(jnp.int32, self.dots.shape, 1)
-        low_half = lax.broadcasted_iota(jnp.int32, (PATCHES, LANES), 1) < size
-        low_table = lax.broadcasted_iota(jnp.int32, (table, LANES), 1) < size
         right = self.rights[SHARED]
-        self.grad_dots[...] = jnp.zeros_like(self.grad_dots)
-        self.grad_pixels[...] = jnp.zeros_like(self.grad_pixels)
+
+        def clear():
+            self.grad_dots[...] = jnp.zeros_like(self.grad_dots)
+            self.grad_pixels[...] = jnp.zeros_like(self.grad_pixels)
+
+        self.do(clear)
         slabs = [pl.ds(p * VARS, VARS) for p in range(PATCH_PIXELS + 1)]
 
         def pair(g):
+            lane = lax.broadcasted_iota(jnp.int32, self.dots.shape, 1)
+            low_half = lax.broadcasted_iota(jnp.int32, (PATCHES, LANES), 1) < size
+            low_table = lax.broadcasted_iota(jnp.int32, (table, LANES), 1) < size
             column = pl.multiple_of(g * LANES, LANES)
             values = self.values[:, pl.ds(column, LANES)]
             grad = self.narrow_grad[:, pl.ds(column, LANES)]
@@ -609,19 +671,23 @@
             found = jnp.where(low_table, halves[0], halves[1]).astype(jnp.bfloat16)
             right[pl.ds(0, table), pl.ds(2 * D + column, LANES)] = found
 
-        self.loop(HEADS // 2, pair)
-        unit = lax.broadcasted_iota(jnp.int32, (D, LANES), 0)
-        head_first = lax.broadcasted_iota(jnp.int32, (D, LANES), 1) * size
-        member = jnp.where((unit >= head_first) & (unit < head_first + size), 1.0, 0.0)
-        wide = mul(self.grad_dots[...], member, ((1,), (1,)), highest_precision)
-        query = jnp.sum(wide * self.keys[...], 0, keepdims=True)
-        depth = right.shape[0]
-        right[pl.ds(0, table), pl.ds(0, D)] = jnp.zeros((table, D), jnp.bfloat16)
-        right[pl.ds(0, table), pl.ds(D, D)] = (wide * self.rows[VEC_ROWS : VEC_ROWS + 1, :]).astype(jnp.bfloat16)
-        first = lax.broadcasted_iota(jnp.int32, (depth - table, D), 0) == 0
-        right[pl.ds(table, depth - table), pl.ds(0, D)] = jnp.where(first, query, 0.0).astype(jnp.bfloat16)
-        right[pl.ds(table, depth - table), pl.ds(D, 2 * D)] = jnp.zeros((depth - table, 2 * D), jnp.bfloat16)
-        self.grad_rows[VEC_ROWS : VEC_ROWS + 1, :] = query
+        self.loop(HEADS // 2, pair, 8)
+
+        def widen():
+            unit = lax.broadcasted_iota(jnp.int32, (D, LANES), 0)
+            head_first = lax.broadcasted_iota(jnp.int32, (D, LANES), 1) * size
+            member = jnp.where((unit >= head_first) & (unit < head_first + size), 1.0, 0.0)
+            wide = mul(self.grad_dots[...], member, ((1,), (1,)), highest_precision)
+            query = jnp.sum(wide * self.keys[...], 0, keepdims=True)
+            depth = right.shape[0]
+            right[pl.ds(0, table), pl.ds(0, D)] = jnp.zeros((table, D), jnp.bfloat16)
+            right[pl.ds(0, table), pl.ds(D, D)] = (wide * self.rows[VEC_ROWS : VEC_ROWS + 1, :]).astype(jnp.bfloat16)
+            first = lax.broadcasted_iota(jnp.int32, (depth - table, D), 0) == 0
+            right[pl.ds(table, depth - table), pl.ds(0, D)] = jnp.where(first, query, 0.0).astype(jnp.bfloat16)
+            right[pl.ds(table, depth - table), pl.ds(D, 2 * D)] = jnp.zeros((depth - table, 2 * D), jnp.bfloat16)
+            self.grad_rows[VEC_ROWS : VEC_ROWS + 1, :] = query
+
+        self.do(widen)
 
     def small(self):
         devices = self.devices
@@ -634,35 +700,44 @@
 
         def one(column, weight):
             back = mul(right[pl.ds(0, table), pl.ds(D, 2 * D)], weight(D, 2 * D), ((1,), (1,)))
+            for c in range(TILE // LANES):
+                self.table_grad[column // LANES + c] = back[:, c * LANES : (c + 1) * LANES]
             query = jnp.broadcast_to(self.grad_rows[VEC_ROWS : VEC_ROWS + 1, :], (8, D))
             row = mul(query, weight(0, D).astype(jnp.float32), ((1,), (1,)), highest_precision)
-            self.grad_rows[0:1, column : column + TILE] = row[0:1]
-            for p in range(PATCH_PIXELS + 1):
-                for b in range(period):
-                    for c in range(TILE // LANES):
-                        line = ((PATCH_PIXELS + 1) * b + p) * per_row + column // LANES + c
-                        start = tall * (line // each) + line % each
-                        first = p * VARS + b * count
-                        self.lines[pl.ds(start, count, stride=tall * span), :] = back[
-                            first : first + count, c * LANES : (c + 1) * LANES
-                        ]
-
-        self.row_tiles(SHARED, one, True)
-        first, each = each, VEC_ROWS * per_row // devices
-        for row in range(VEC_ROWS):
-            for c in range(per_row):
-                line = row * per_row + c
-                start = tall * (line // each) + first + line % each
-                self.lines[pl.ds(start, 1), :] = self.grad_rows[pl.ds(row, 1), pl.ds(c * LANES, LANES)]
-        first, rows = first + each, PATCHES // devices
-        for row in range(rows):
-            for c in range(per_row):
-                start = first + row * per_row + c
-                self.lines[pl.ds(start, devices, stride=tall), :] = self.positions[
-                    c, pl.ds(row, devices, stride=rows), :
-                ]
-        for line in range(first + rows * per_row, tall):
-            self.lines[pl.ds(line, devices, stride=tall), :] = jnp.zeros((devices, LANES), jnp.float32)
+            self.grad_rows[0:1, pl.ds(column, TILE)] = row[0:1]
+
+        self.row_tiles(SHARED, one)
+
+        def table_lines(p):
+            for b in range(period):
+                for c in range(per_row):
+                    line = ((PATCH_PIXELS + 1) * b + p) * per_row + c
+                    start = tall * (line // each) + line % each
+                    self.lines[pl.ds(start, count, stride=tall * span), :] = self.table_grad[
+                        c, pl.ds(p * VARS + b * count, count), :
+                    ]
+
+        for p in range(PATCH_PIXELS + 1):
+            self.do(functools.partial(table_lines, p))
+        of_vectors = VEC_ROWS * per_row // devices
+
+        def rest():
+            for row in range(VEC_ROWS):
+                for c in range(per_row):
+                    line = row * per_row + c
+                    start = tall * (line // of_vectors) + each + line % of_vectors
+                    self.lines[pl.ds(start, 1), :] = self.grad_rows[pl.ds(row, 1), pl.ds(c * LANES, LANES)]
+            first, rows = each + of_vectors, PATCHES // devices
+            for row in range(rows):
+                for c in range(per_row):
+                    start = first + row * per_row + c
+                    self.lines[pl.ds(start, devices, stride=tall), :] = self.positions[
+                        c, pl.ds(row, devices, stride=rows), :
+                    ]
+            for line in range(first + rows * per_row, tall):
+                self.lines[pl.ds(line, devices, stride=tall), :] = jnp.zeros((devices, LANES), jnp.float32)
+
+        self.do(rest)
 
         cores = self.pack.shape[0]
 
@@ -683,6 +758,9 @@
 
 
 LOADED = (0, 2, 3, 4, 5, 6)
+SHIPPED = {0: (0, 1, 2, 3, 4, 5, 6), 1: (7, 8), 2: (9, 10, 11, 12, 13), 4: (14, 15)}
+GATHER_CHUNKS = 3
+SCATTER_CHUNKS = 2
 
 
 def forward_shapes():
@@ -721,10 +799,12 @@
         return found
 
     flats, given = take(kinds), take(2 if fused else 0)
-    whole, outs = take(kinds), take(len(forward_shapes()) if fused else 0)
-    shards = take(kinds)
+    results = len(forward_shapes()) if fused else 0
+    whole, targets = take(kinds), take(results)
+    shards, outs = take(kinds), take(results)
     loaded = dict(zip(LOADED, take(len(LOADED) if fused else 0)))
     scratch = take(9 if fused else 0)
+    ship_sem = take(1 if fused else 0)
     load_sem = take(1 if fused else 0)
     single, send_sem, relay_sem, recv_sem, own_sem = refs
     forward = Forward(wide * narrow, loaded, loaded[6], given, outs, scratch) if fused else None
@@ -915,20 +995,31 @@
                 settle_own(part[1])
                 load(part).start()
 
+    def ship(i):
+        return pltpu.make_async_copy(outs[i], targets[i], ship_sem[0].at[i])
+
     def stage_compute(parts):
-        for part in parts:
-            if fused and part[1] in LOADED:
-                load(part).wait()
         if fused:
-            for work in forward.after(phases.index(parts)):
-                work()
+            for part in parts:
+                if part[1] in LOADED:
+                    forward.do(lambda part=part: load(part).wait())
+            for plan in forward.after(phases.index(parts)):
+                plan()
+            for i in SHIPPED.get(phases.index(parts), ()):
+                forward.do(ship(i).start)
 
     stages = (send_own, stage_b, stage_c, stage_d, stage_e, stage_f, stage_load, stage_compute)
-    lags = (0, 1, 2, 3, 4, 5, 5, 6)
+    lags = (0, 2, 2, 3, 3, 4, 4, 5)
     for step in range(len(phases) + lags[-1]):
-        for stage in (5, 4, 3, 2, 1, 0, 6, 7):
+        for stage in (5, 3, 1, 0, 4, 2, 6, 7):
             if 0 <= step - lags[stage] < len(phases):
                 stages[stage](phases[step - lags[stage]])
+                if fused:
+                    forward.run(GATHER_CHUNKS)
+    if fused:
+        forward.run(len(forward.chunks))
+        for i in range(results):
+            ship(i).wait()
     for kind in range(kinds):
         settle_own(kind)
         sent = whole[kind].at[pl.ds(0, here.devices - PLANES)]
@@ -952,6 +1043,7 @@
     parts = sum(len(phase) for phase in phase_parts(widths, devices, PHASES, COARSE_PHASES))
     results = forward_shapes() if fused else []
     scratch = [pltpu.VMEM(s, f.dtype) for s, f in zip(shapes, flats)]
+    scratch += [pltpu.VMEM(r.shape, r.dtype) for r in results]
     if fused:
         scratch += [pltpu.VMEM((devices,) + shapes[kind], flats[kind].dtype) for kind in LOADED]
         scratch += [
@@ -964,6 +1056,7 @@
             pltpu.VMEM((PATCHES, D), jnp.bfloat16),
             pltpu.VMEM((PATCHES, D), jnp.bfloat16),
             pltpu.VMEM((PATCHES, D), jnp.bfloat16),
+            pltpu.SemaphoreType.DMA((len(results),)),
             pltpu.SemaphoreType.DMA((parts,)),
         ]
     scratch += [
@@ -977,8 +1070,7 @@
         functools.partial(gather_kernel, widths, wide, narrow, fused),
         out_shape=[jax.ShapeDtypeStruct((devices,) + s, f.dtype) for s, f in zip(shapes, flats)] + results,
         in_specs=[pl.BlockSpec(memory_space=pltpu.VMEM)] * (kinds + len(given)),
-        out_specs=[pl.BlockSpec(memory_space=pl.ANY)] * kinds
-        + [pl.BlockSpec(memory_space=pltpu.VMEM)] * len(results),
+        out_specs=[pl.BlockSpec(memory_space=pl.ANY)] * (kinds + len(results)),
         scratch_shapes=scratch,
         compiler_params=pltpu.CompilerParams(
             collective_id=0, has_side_effects=True, vmem_limit_bytes=VMEM_BYTES
@@ -1039,7 +1131,8 @@
 
 
 BACK_GIVEN = 11
-BACK_SCRATCH = 13
+FIRST_GIVEN = (10, 0, 8)
+BACK_SCRATCH = 14
 
 
 def scatter_kernel(direct, shapes, wide, narrow, fused, *refs):
@@ -1055,17 +1148,28 @@
         inputs = [take(2) if kind == 1 else take(1) if direct[kind] else [] for kind in range(kinds)]
     else:
         inputs = [take(2) if direct[kind] else take(1) for kind in range(kinds)]
-    weights, streamed, given = (take(count if fused else 0) for count in (6, 2, BACK_GIVEN))
+    weights, streamed, sources = (take(count if fused else 0) for count in (6, 2, BACK_GIVEN))
     sums = take(kinds)
     outs = take(2 if fused else 0)
     own, second, first, planes, cross = (take(kinds) for _ in range(5))
     local = [take(3) if direct[kind] and kind == SHARED else take(2) if direct[kind] else take(1) for kind in range(kinds)]
     scratch = take(BACK_SCRATCH if fused else 0)
+    given = take(BACK_GIVEN if fused else 0)
+    given_sem = take(1 if fused else 0)
     send_sem, near_send_sem, own_sem, near_sem, second_sem, first_sem, plane_sem, cross_sem = refs
     backward = None
     if fused:
         inputs[6] = [scratch[0]]
         rights = [local[kind][1] if direct[kind] else None for kind in range(kinds)]
+        bring = [
+            pltpu.make_async_copy(source, target, given_sem[0].at[i])
+            for i, (source, target) in enumerate(zip(sources, given))
+        ]
+        for i in FIRST_GIVEN:
+            bring[i].start()
+        for i in range(BACK_GIVEN):
+            if i not in FIRST_GIVEN:
+                bring[i].start()
         backward = Backward(wide * narrow, narrow, weights, streamed, given, outs, rights, scratch)
     here = Place(wide, narrow)
     here.greet()
@@ -1282,18 +1386,38 @@
         place = (here.z - z + PLANES) % PLANES - 1
         send(part, slot, planes, place, plane_sem, here.address(z, here.y, here.x, here.core))
 
-    seen = set()
-    for kind in (1, 0, 5, 3, 4, 2, 6):
+    seen, made, plans = set(), set(), {}
+    fetch_left(1)
+    fetch_right(1)
+    for kind in (0, 5, 3, 4, 2, 6):
         fetch_left(kind)
 
+    def hand_on(kind):
+        fetch_right(kind)
+        made.add(kind)
+
+    if fused:
+        for phase in range(len(phases)):
+            works, plans[phase] = backward.before(phase)
+            if phase == 2:
+                for i in FIRST_GIVEN:
+                    backward.do(bring[i].wait)
+            if phase == 4:
+                for i in range(BACK_GIVEN):
+                    if i not in FIRST_GIVEN:
+                        backward.do(bring[i].wait)
+            for work in works:
+                work()
+            for kind in plans[phase]:
+                backward.do(functools.partial(hand_on, kind))
+
     def stage_fetch(parts):
-        works, ready_kinds = backward.before(phases.index(parts)) if fused else ((), ())
-        for work in works:
-            work()
+        ready_kinds = plans[phases.index(parts)] if fused else ()
         for kind in ready_kinds:
-            fetch_right(kind)
+            while kind not in made:
+                backward.run(1)
         for part in parts:
-            if part[1] not in seen and part[1] not in ready_kinds and not (fused and part[1] != 1):
+            if part[1] not in seen and part[1] != 1 and not fused:
                 fetch_right(part[1])
             seen.add(part[1])
 
@@ -1311,12 +1435,12 @@
         for part in parts:
             b_count = axes(part)[3]
             a_count = axes(part)[2]
+            loop(2, lambda i: far_pairs(part, lambda p, q: to_second(part, plane_in_order(2 + i), p, q, True)))
             loop(
                 4,
                 lambda i: repeat(b_count - 1, lambda j: to_second(part, plane_in_order(i), 0, 1 + j, False)),
             )
             loop(2, lambda i: repeat(a_count - 1, lambda j: to_first(part, plane_in_order(i), 1 + j, False)))
-            loop(2, lambda i: far_pairs(part, lambda p, q: to_second(part, plane_in_order(2 + i), p, q, True)))
 
     def stage_first(parts):
         for part in parts:
@@ -1338,6 +1462,8 @@
         for lag, stage in reversed(list(enumerate(stages))):
             if 0 <= step - lag < len(phases):
                 stage(phases[step - lag])
+                if fused:
+                    backward.run(SCATTER_CHUNKS)
     for kind in range(kinds):
         for copy in (theirs_left(kind) if direct[kind] else []) + theirs_right(kind):
             copy.wait_send()
@@ -1413,8 +1539,11 @@
             pltpu.VMEM((VARS * (PATCH_PIXELS + 1), LANES), full),
             pltpu.VMEM((D // LANES, PATCHES, LANES), full),
             pltpu.VMEM((devices * shapes[6][0], LANES), full),
+            pltpu.VMEM((D // LANES, VARS * (PATCH_PIXELS + 1), LANES), full),
             pltpu.SemaphoreType.DMA((2, 3)),
         ]
+        scratch += [pltpu.VMEM(g.shape, g.dtype) for g in given]
+        scratch.append(pltpu.SemaphoreType.DMA((len(given),)))
     widths = [s[1] for s in shapes]
     parts = sum(len(phase) for phase in phase_parts(widths, devices, SUM_PHASES, COARSE_SUM_PHASES))
     scratch += [pltpu.SemaphoreType.DMA((kinds,))] + [pltpu.SemaphoreType.DMA((kinds, 2))] * 3
@@ -1423,8 +1552,7 @@
     found = pl.pallas_call(
         functools.partial(scatter_kernel, tuple(direct), tuple(shapes), wide, narrow, fused),
         out_shape=[jax.ShapeDtypeStruct((s[0] * s[1] // LANES, LANES), jnp.float32) for s in shapes] + outs,
-        in_specs=[pl.BlockSpec(memory_space=pl.ANY)] * len(operands)
-        + [pl.BlockSpec(memory_space=pltpu.VMEM)] * len(given),
+        in_specs=[pl.BlockSpec(memory_space=pl.ANY)] * (len(operands) + len(given)),
         out_specs=[pl.BlockSpec(memory_space=pltpu.VMEM)] * (kinds + len(outs)),
         scratch_shapes=scratch,
         compiler_params=pltpu.CompilerParams(
@@ -1435,17 +1563,22 @@
     return found[:kinds], found[kinds:]
 
 
-def hand_over_kernel(*refs):
-    for source, target in zip(refs[: len(refs) // 2], refs[len(refs) // 2 :]):
+def hand_over_kernel(count, *refs):
+    for source, target in zip(refs[: count - 1], refs[count:]):
         target[...] = source[...]
-
-
-def hand_over(arrays):
+    first = 0
+    for target in refs[2 * count - 1 :]:
+        target[...] = refs[count - 1][first : first + target.shape[0], :]
+        first += target.shape[0]
+
+
+def hand_over(arrays, sizes):
+    shapes = [a.shape for a in arrays[:-1]] + [(size // LANES, LANES) for size in sizes]
     return pl.pallas_call(
-        hand_over_kernel,
-        out_shape=[jax.ShapeDtypeStruct(a.shape, a.dtype) for a in arrays],
+        functools.partial(hand_over_kernel, len(arrays)),
+        out_shape=[jax.ShapeDtypeStruct(shape, arrays[0].dtype) for shape in shapes],
         in_specs=[pl.BlockSpec(memory_space=pltpu.VMEM)] * len(arrays),
-        out_specs=[pl.BlockSpec(memory_space=pltpu.VMEM)] * len(arrays),
+        out_specs=[pl.BlockSpec(memory_space=pltpu.VMEM)] * len(shapes),
         name="hand_over",
     )(*arrays)
 
@@ -1786,20 +1919,23 @@
             narrow,
         )
     if fused:
-        summed = hand_over(summed)
-    flat_small = summed[6].reshape(-1)
+        summed = hand_over(summed, [s.size for s in small])
+        small_sums = [part.reshape(-1) for part in summed[6:]]
+    else:
+        flat_small = summed[6].reshape(-1)
+        small_sums = [flat_small[:cut_one], flat_small[cut_one:cut_two], flat_small[cut_two:cut_three]]
     return (
         result[None],
         fields_grad[None],
-        flat_small[:cut_one],
+        small_sums[0],
         summed[2].reshape(-1),
         summed[4].reshape(-1),
         summed[3].reshape(-1),
         summed[5].reshape(-1),
         summed[0].reshape(-1),
         summed[1].reshape(-1),
-        flat_small[cut_one:cut_two],
-        flat_small[cut_two:cut_three],
+        small_sums[1],
+        small_sums[2],
     )
 
 

time: 348 us -> 320 us (0.920)
  Pallas kernels: 331 us -> 308 us
  local copies, waits for them, and re-layouts: 8.43 us -> 3.66 us
    pallas_call x1, Pallas kernels: 172 us -> 152 us  [scatter_all(): pl.pallas_call(functools.partial(scatter_kernel, tuple(direct), tuple(sha...]
    slice x3 -> x0, local copies, waits for them, and re-layouts: 3.97 us -> none  [the longest x1 1.37 us: on_device(): flat_small[:cut_one]]
where the time goes in v1:
time: 320 us; the launch traced here: 317 us
  Pallas kernels  308 us (96%)
  local copies, waits for them, and re-layouts  3.66 us (1%)
    pallas_call x1, Pallas kernels, gather_all(): pl.pallas_call(functools.partial(gather_kernel, widths, wide, narrow, fus...  153 us
    pallas_call x1, Pallas kernels, scatter_all(): pl.pallas_call(functools.partial(scatter_kernel, tuple(direct), tuple(sha...  152 us

profile of v1, /device:TPU:8, one launch (start us, length us, event | category | flops | bytes accessed | tf_op | source)
XLA Modules:
  0.0 316.9 jit_solution(5340475954631000795)
XLA Ops:
  0.6 0.9 convolution_bitcast_fusion.1
  1.5 1.4 maximum_bitcast_fusion.refs_6_
  2.9 0.7 broadcast_in_dim.18.refs_8_
  3.6 1.1 convolution_bitcast_fusion
  4.7 0.7 concatenate.7
  5.3 152.9 %gather_all.1 = (bf16[32,32,4096]{2,1,0:T(8,128)(2,1)}, bf16[32,128,1024]{2,1,0:T(8,128)(2,1)}, bf16[32,32,3072]{2,1,0:T(8,128)(2,1)}, bf16[32,32,3072]{2,1,0:T(...) custom-call(bf16[1024,128]{1,0:T(8,128)(2,1)} %bitcast.55, ...), custom_call_target="tpu_custom_call" | custom-call | tf_op jit(solution)/shard_map/gather_all/pallas_call | solution.py:1069
  158.2 0.0 copy-start
  158.2 0.0 copy-start.1
  158.3 152.3 %scatter_all.1 = (f32[1024,128]{1,0:T(8,128)}, f32[1024,128]{1,0:T(8,128)}, f32[768,128]{1,0:T(8,128)}, f32[768,128]{1,0:T(8,128)}, f32[256,128]{1,0:T(8,128)}, ...) custom-call(bf16[8,2,64,128]{3,2,1,0:T(8,128)(2,1)} %bitcast.54, ...), custom_call_target="tpu_custom_call" | custom-call | tf_op jit(solution)/shard_map/scatter_all/pallas_call | solution.py:1552
  310.6 0.9 convert_element_type.18
  311.5 0.0 copy-done
  311.5 0.0 copy-done.1
  311.5 0.2 fusion
  311.7 0.6 copy.27
  312.4 2.8 hand_over.1
  315.2 1.7 copy.33
  (1 shorter events, 0.0 us)
Async XLA Ops:
  158.2 153.3 %copy-start = (s32[1,48]{1,0:T(1,128)S(1)}, s32[1,48]{1,0:T(1,128)}, u32[]{:S(2)}) copy-start(s32[1,48]{1,0:T(1,128)} %param.15) | copy-start | bytes 580
  158.2 153.3 %copy-start.1 = (s32[48]{0:T(128)S(1)}, s32[48]{0:T(128)}, u32[]{:S(2)}) copy-start(s32[48]{0:T(128)} %constant.6.clone) | copy-start | bytes 580

commit v2 on v1

--- a/solution.py
+++ b/solution.py
@@ -809,16 +809,24 @@
     single, send_sem, relay_sem, recv_sem, own_sem = refs
     forward = Forward(wide * narrow, loaded, loaded[6], given, outs, scratch) if fused else None
     here = Place(wide, narrow)
-    for kind in range(kinds):
-        lines_to_rows(flats[kind], single, shards[kind])
-    here.greet()
     own_slot = here.block(here.z, here.y, here.x, here.core)
-    for kind in range(kinds):
-        pltpu.make_async_copy(shards[kind], whole[kind].at[own_slot], own_sem.at[kind]).start()
+    laid = set()
+
+    def lay_out(parts):
+        for part in parts:
+            kind = part[1]
+            if kind not in laid:
+                lines_to_rows(flats[kind], single, shards[kind])
+                pltpu.make_async_copy(shards[kind], whole[kind].at[own_slot], own_sem.at[kind]).start()
+            laid.add(kind)
+
     phases, number = [], 0
     for parts in phase_parts(widths, here.devices, PHASES, COARSE_PHASES):
         phases.append([(number + i,) + part for i, part in enumerate(parts)])
         number += len(parts)
+
+    lay_out(phases[0])
+    here.greet()
 
     def view(part, slot):
         kind, at, width = part[1:4]
@@ -884,6 +892,9 @@
             relay(part, own_slot, beside, source)
             pl.when(middle)(lambda part=part, source=source: relay(part, own_slot, facing, source))
             to_sibling(part, own_slot, source)
+        following = phases.index(parts) + 1
+        if following < len(phases):
+            lay_out(phases[following])
 
     def first_hop(parts, z, passes=True):
         slot = here.block(z, here.y, here.x, here.core)
@@ -1009,9 +1020,9 @@
                 forward.do(ship(i).start)
 
     stages = (send_own, stage_b, stage_c, stage_d, stage_e, stage_f, stage_load, stage_compute)
-    lags = (0, 2, 2, 3, 3, 4, 4, 5)
+    lags = (0, 2, 3, 4, 5, 6, 6, 7)
     for step in range(len(phases) + lags[-1]):
-        for stage in (5, 3, 1, 0, 4, 2, 6, 7):
+        for stage in (5, 4, 3, 2, 1, 0, 6, 7):
             if 0 <= step - lags[stage] < len(phases):
                 stages[stage](phases[step - lags[stage]])
                 if fused:

time: 320 us -> 318 us (level)
  no operation moved by 1% of the time
where the time goes in v2:
time: 318 us; the launch traced here: 316 us
  Pallas kernels  307 us (97%)
  local copies, waits for them, and re-layouts  3.66 us (1%)
    pallas_call x1, Pallas kernels, scatter_all(): pl.pallas_call(functools.partial(scatter_kernel, tuple(direct), tuple(sha...  153 us
    pallas_call x1, Pallas kernels, gather_all(): pl.pallas_call(functools.partial(gather_kernel, widths, wide, narrow, fus...  150 us

profile of v2, /device:TPU:8, one launch (start us, length us, event | category | flops | bytes accessed | tf_op | source)
XLA Modules:
  0.0 315.5 jit_solution(2077829091582927749)
XLA Ops:
  0.6 0.9 convolution_bitcast_fusion.1
  1.5 1.4 maximum_bitcast_fusion.refs_6_
  2.9 0.7 broadcast_in_dim.18.refs_8_
  3.6 1.1 convolution_bitcast_fusion
  4.7 0.7 concatenate.7
  5.3 150.5 %gather_all.1 = (bf16[32,32,4096]{2,1,0:T(8,128)(2,1)}, bf16[32,128,1024]{2,1,0:T(8,128)(2,1)}, bf16[32,32,3072]{2,1,0:T(8,128)(2,1)}, bf16[32,32,3072]{2,1,0:T(...) custom-call(bf16[1024,128]{1,0:T(8,128)(2,1)} %bitcast.55, ...), custom_call_target="tpu_custom_call" | custom-call | tf_op jit(solution)/shard_map/gather_all/pallas_call | solution.py:1080
  155.8 0.0 copy-start
  155.8 0.0 copy-start.1
  155.8 153.4 %scatter_all.1 = (f32[1024,128]{1,0:T(8,128)}, f32[1024,128]{1,0:T(8,128)}, f32[768,128]{1,0:T(8,128)}, f32[768,128]{1,0:T(8,128)}, f32[256,128]{1,0:T(8,128)}, ...) custom-call(bf16[8,2,64,128]{3,2,1,0:T(8,128)(2,1)} %bitcast.54, ...), custom_call_target="tpu_custom_call" | custom-call | tf_op jit(solution)/shard_map/scatter_all/pallas_call | solution.py:1563
  309.3 0.9 convert_element_type.18
  310.2 0.0 copy-done
  310.2 0.0 copy-done.1
  310.2 0.2 fusion
  310.4 0.6 copy.27
  311.0 2.8 hand_over.1
  313.9 1.7 copy.33
  (1 shorter events, 0.0 us)
Async XLA Ops:
  155.8 154.3 %copy-start = (s32[1,48]{1,0:T(1,128)S(1)}, s32[1,48]{1,0:T(1,128)}, u32[]{:S(2)}) copy-start(s32[1,48]{1,0:T(1,128)} %param.15) | copy-start | bytes 580
  155.8 154.3 %copy-start.1 = (s32[48]{0:T(128)S(1)}, s32[48]{0:T(128)}, u32[]{:S(2)}) copy-start(s32[48]{0:T(128)} %constant.6.clone) | copy-start | bytes 580

commit v3 on v2

--- a/solution.py
+++ b/solution.py
@@ -1020,9 +1020,9 @@
                 forward.do(ship(i).start)
 
     stages = (send_own, stage_b, stage_c, stage_d, stage_e, stage_f, stage_load, stage_compute)
-    lags = (0, 2, 3, 4, 5, 6, 6, 7)
+    lags = (0, 2, 3, 4, 5, 6, 6, 6)
     for step in range(len(phases) + lags[-1]):
-        for stage in (5, 4, 3, 2, 1, 0, 6, 7):
+        for stage in (5, 6, 4, 3, 2, 1, 0, 7):
             if 0 <= step - lags[stage] < len(phases):
                 stages[stage](phases[step - lags[stage]])
                 if fused:

time: 318 us -> 312 us (0.981)
  Pallas kernels: 307 us -> 300 us
    pallas_call x1, Pallas kernels: 150 us -> 144 us  [gather_all(): pl.pallas_call(functools.partial(gather_kernel, widths, wide, narrow, fus...]
where the time goes in v3:
time: 312 us; the launch traced here: 309 us
  Pallas kernels  300 us (96%)
  local copies, waits for them, and re-layouts  3.66 us (1%)
    pallas_call x1, Pallas kernels, scatter_all(): pl.pallas_call(functools.partial(scatter_kernel, tuple(direct), tuple(sha...  153 us
    pallas_call x1, Pallas kernels, gather_all(): pl.pallas_call(functools.partial(gather_kernel, widths, wide, narrow, fus...  144 us

profile of v3, /device:TPU:8, one launch (start us, length us, event | category | flops | bytes accessed | tf_op | source)
XLA Modules:
  0.0 308.7 jit_solution(17329821729141425102)
XLA Ops:
  0.6 0.9 convolution_bitcast_fusion.1
  1.5 1.4 maximum_bitcast_fusion.refs_6_
  2.9 0.7 broadcast_in_dim.18.refs_8_
  3.6 1.1 convolution_bitcast_fusion
  4.7 0.7 concatenate.7
  5.3 144.3 %gather_all.1 = (bf16[32,32,4096]{2,1,0:T(8,128)(2,1)}, bf16[32,128,1024]{2,1,0:T(8,128)(2,1)}, bf16[32,32,3072]{2,1,0:T(8,128)(2,1)}, bf16[32,32,3072]{2,1,0:T(...) custom-call(bf16[1024,128]{1,0:T(8,128)(2,1)} %bitcast.55, ...), custom_call_target="tpu_custom_call" | custom-call | tf_op jit(solution)/shard_map/gather_all/pallas_call | solution.py:1080
  149.7 0.0 copy-start
  149.7 0.0 copy-start.1
  149.7 152.8 %scatter_all.1 = (f32[1024,128]{1,0:T(8,128)}, f32[1024,128]{1,0:T(8,128)}, f32[768,128]{1,0:T(8,128)}, f32[768,128]{1,0:T(8,128)}, f32[256,128]{1,0:T(8,128)}, ...) custom-call(bf16[8,2,64,128]{3,2,1,0:T(8,128)(2,1)} %bitcast.54, ...), custom_call_target="tpu_custom_call" | custom-call | tf_op jit(solution)/shard_map/scatter_all/pallas_call | solution.py:1563
  302.5 0.9 convert_element_type.18
  303.4 0.0 copy-done
  303.4 0.0 copy-done.1
  303.4 0.2 fusion
  303.6 0.6 copy.27
  304.2 2.8 hand_over.1
  307.1 1.7 copy.33
  (1 shorter events, 0.0 us)
Async XLA Ops:
  149.7 153.7 %copy-start = (s32[1,48]{1,0:T(1,128)S(1)}, s32[1,48]{1,0:T(1,128)}, u32[]{:S(2)}) copy-start(s32[1,48]{1,0:T(1,128)} %param.15) | copy-start | bytes 580
  149.7 153.7 %copy-start.1 = (s32[48]{0:T(128)S(1)}, s32[48]{0:T(128)}, u32[]{:S(2)}) copy-start(s32[48]{0:T(128)} %constant.6.clone) | copy-start | bytes 580
